TPU v7x, 32 devices: a whole 2x2x4 slice. The times are simulated.
32 devices in a mesh: span: 8 (over z, y), plane: 4 (over x, core).
Axes of the slice: x: 2, y: 2, z: 4, core: 2. Of those that a mesh axis runs over, the one named last changes fastest.
Arguments:
- adjoint: float32 [3, 32, 81, 512], P(None, 'span', None, 'plane'), may hold values from -6 to 6
- checkpoints: bfloat16 [8, 2, 32, 81, 512], P(None, None, 'span', None, 'plane'), may hold values from -4 to 4
- checkpoint_step: int32 [3], replicated, may hold values from 0 to 7
- metric: float32 [2, 512], P(None, 'plane'), may hold values from 0.004 to 0.016
- helmholtz_inverse: float32 [32, 81, 81], P('span'), may hold values from -0.08 to 0.8
- wall_element: int32 [1024, 2], replicated, may hold values from 0 to 511
- wall_local: int32 [1024, 2], replicated, may hold values from 0 to 80
- wall_weight: float32 [32, 1024], P('span'), may hold values from 0.7 to 140
Outputs:
- adjoint_next: float32 [3, 32, 81, 512], P(None, 'span', None, 'plane')
- control_gradient: float32 [32, 1024], P('span', 'plane')
All inputs are finite; a program needn't handle non-finite values.
Results may differ from a plain program's by a relative error of at most 0.00065.
Values may be sent and summed in bfloat16 or wider, within the bound.
A program may use at most 128 MiB of HBM per device.

v0:
```python
import functools

import jax
import jax.numpy as jnp
import ml_dtypes
import numpy as np
from jax import lax
from jax.experimental import pallas as pl
from jax.experimental.pallas import tpu as pltpu
from jax.sharding import PartitionSpec as P

P_SIZE = 8
NSTEP = 3


HIGHEST = lax.Precision.HIGHEST


def chebyshev_matrix(degree):
    points = np.arange(degree + 1)
    abscissa = np.cos(np.pi * points / degree)
    signed = np.where((points == 0) | (points == degree), 2.0, 1.0) * (-1.0) ** points
    spacing = abscissa[:, None] - abscissa[None, :] + np.eye(degree + 1)
    matrix = signed[:, None] / signed[None, :] / spacing
    return matrix - np.eye(degree + 1) * np.sum(matrix, axis=1)[:, None]


def fourier_table(length):
    row_index = np.arange(length)[:, None]
    column = np.arange(length)[None, :]
    wavenumber = (row_index + 1) // 2
    phase_angle = 2.0 * np.pi * wavenumber * column / length
    parity = row_index % 2
    base_rows = np.where(
        row_index == 0, 1.0, np.where(parity == 1, np.cos(phase_angle), np.sin(phase_angle))
    )
    row_scale = np.where(
        (row_index == 0) | (row_index == length - 1), 1.0 / np.sqrt(length), np.sqrt(2.0 / length)
    )
    return base_rows * row_scale


def transport(field_data, velocity, metric):
    side_nodes = P_SIZE + 1
    matrix = jnp.asarray(chebyshev_matrix(P_SIZE), jnp.float32)
    shaped = field_data.reshape(
        field_data.shape[0], field_data.shape[1], side_nodes, side_nodes, field_data.shape[3]
    )
    first_dir = jnp.einsum("ai,czibe->czabe", matrix, shaped, precision=HIGHEST).reshape(
        field_data.shape
    )
    second_dir = jnp.einsum("bi,czaie->czabe", matrix, shaped, precision=HIGHEST).reshape(
        field_data.shape
    )
    speed_data = velocity.astype(jnp.float32)
    return (
        field_data
        + speed_data[0] * (metric[0] * first_dir)
        + speed_data[1] * (metric[1] * second_dir)
    )


def forward_modes(gathered):
    basis_table = jnp.asarray(fourier_table(gathered.shape[1]), jnp.float32)
    return jnp.einsum("jz,czqe->cjqe", basis_table, gathered, precision=HIGHEST)


def backward_planes(solved):
    basis_table = jnp.asarray(fourier_table(solved.shape[1]), jnp.float32)
    return jnp.einsum("jz,cjqe->czqe", basis_table, solved, precision=HIGHEST)


def solve_modes(inverse_block, coefficients):
    return jnp.einsum("jqr,cjre->cjqe", inverse_block, coefficients, precision=HIGHEST)


def to_plane_layout(point_data):
    return lax.all_to_all(point_data, "span", split_axis=1, concat_axis=3, tiled=True)


def wall_terms(field_one, speed_one, flat_index, inside, wall_count):
    rows = field_one.shape[0]
    values = jnp.take(field_one.reshape(rows, -1), flat_index, axis=1)
    speeds = jnp.take(speed_one.reshape(rows, -1), flat_index, axis=1).astype(jnp.float32)
    product = jnp.where(inside, values * speeds, 0.0).reshape(rows, wall_count, 2)
    return jnp.sum(product, axis=2)


def on_device(
    adjoint,
    checkpoints,
    checkpoint_step,
    metric,
    helmholtz_inverse,
    wall_element,
    wall_local,
    wall_weight,
):
    planes_dev = adjoint.shape[1]
    elems_dev = adjoint.shape[3]
    wall_count = wall_element.shape[0]
    span_count = lax.axis_size("span")
    share = elems_dev // span_count
    all_modes = lax.all_gather(helmholtz_inverse, "span", axis=0, tiled=True)
    offset = lax.axis_index("plane") * elems_dev
    local_element = wall_element - offset
    inside = ((local_element >= 0) & (local_element < elems_dev)).reshape(-1)
    flat_index = (wall_local * elems_dev + jnp.clip(local_element, 0, elems_dev - 1)).reshape(-1)
    velocity = jnp.stack([
        lax.dynamic_index_in_dim(checkpoints, checkpoint_step[s], 0, keepdims=False)
        for s in range(NSTEP)
    ])
    velocity = lax.all_to_all(velocity, "span", split_axis=4, concat_axis=2, tiled=True)
    field = lax.all_to_all(adjoint, "span", split_axis=3, concat_axis=1, tiled=True)
    scale = lax.dynamic_slice_in_dim(metric, lax.axis_index("span") * share, share, 1)
    product = 0.0
    for substep in range(NSTEP):
        advected = transport(field, velocity[substep], scale)
        field = backward_planes(solve_modes(all_modes, forward_modes(advected)))
        product = product + field[1] * velocity[substep, 1].astype(jnp.float32)
    both = to_plane_layout(jnp.concatenate([field, product[None]], axis=0))
    gathered = jnp.take(both[3].reshape(planes_dev, -1), flat_index, axis=1)
    partial_sum = jnp.where(inside, gathered, 0.0).reshape(planes_dev, wall_count, 2).sum(axis=2)
    weighted = wall_weight * partial_sum
    grad_share = lax.psum_scatter(weighted, "plane", scatter_dimension=1, tiled=True)
    square_total = lax.psum(jnp.sum(grad_share * grad_share), ("span", "plane"))
    inverse_rms = lax.rsqrt(square_total / (planes_dev * span_count * wall_count) + 1e-06)
    return (both[:3], grad_share * inverse_rms)


MESH = pl.DeviceIdType.MESH
F32 = jnp.float32
BF16 = jnp.bfloat16
LANES = 128


def swap_blocks(parts, share):
    count = len(parts)
    width = count * share
    lane = lax.broadcasted_iota(jnp.int32, parts[0].shape, 1)
    k = count // 2
    while k:
        upper = (lane // (k * share)) % 2 == 1
        new = list(parts)
        for i in range(count):
            if (i // k) % 2 == 0:
                a, b = parts[i], parts[i + k]
                new[i] = jnp.where(upper, pltpu.roll(b, k * share, 1), a)
                new[i + k] = jnp.where(upper, b, pltpu.roll(a, width - k * share, 1))
        parts = new
        k //= 2
    return parts


def coded(x):
    top = jnp.maximum(jnp.max(jnp.abs(x), axis=0, keepdims=True), 1e-30)
    return jnp.round(x * (32767.0 / top)).astype(jnp.int32), top * (1.0 / 32767.0)


def coded_blocks(rows, sets, half):
    pairs = [coded(rows[i * half:(i + 1) * half]) for i in range(sets)]
    whole = jnp.concatenate([a for a, _ in pairs], axis=0)
    return whole.astype(jnp.int16), [b for _, b in pairs]


def decoded(x, scale):
    return x.astype(jnp.int32).astype(F32) * scale


def greet(spans, planes):
    me, p = lax.axis_index("span"), lax.axis_index("plane")
    barrier = pltpu.get_barrier_semaphore()
    for o in range(1, spans):
        pl.semaphore_signal(barrier, 1, device_id={"span": (me + o) % spans}, device_id_type=MESH)
    for o in range(1, planes):
        pl.semaphore_signal(barrier, 1, device_id={"plane": (p + o) % planes}, device_id_type=MESH)
    pl.semaphore_wait(barrier, spans + planes - 2)


def remote(src, dst, sems, kind, o, target):
    return pltpu.make_async_remote_copy(
        src_ref=src, dst_ref=dst, send_sem=sems.at[0, kind, o], recv_sem=sems.at[1, kind, o],
        device_id=target, device_id_type=MESH,
    )


def step_kernel(spans, planes, zdev, q, qp,
                step_ref, adj_ref, ck_ref, inv_ref, metric_ref, elem_ref, local_ref, weight_ref,
                basis_ref, diff_ref, place_ref,
                back, tback, weighted_ref, trcv,
                xs_ref, vs_ref, padded, inv16, modes_ref, tail, stage, snd, tsnd, rcv, trc, vsnd, vrcv,
                coef, solved, product, modes_cat, bsnd, tbsnd,
                wall, rows_in, part, wrcv, square, srcv, total, sems, local_sem):
    share = LANES // spans
    me, p = lax.axis_index("span"), lax.axis_index("plane")
    bulk = q - 1
    half = bulk // 2
    slabs = 3 * zdev
    sets = 2 * slabs // spans
    greet(spans, planes)

    def span_to(o):
        return {"span": (me + o) % spans}

    eye = (lax.broadcasted_iota(jnp.int32, (qp, LANES), 0)
           == lax.broadcasted_iota(jnp.int32, (qp, LANES), 1))
    padded[...] = jnp.zeros_like(padded)
    extra = []
    for j in range(zdev):
        padded[:q, :q] = inv_ref[:, j, :]
        x = padded[...]
        whole, scale = coded(jnp.where(eye, 0.0, x))
        inv16[j] = whole.astype(jnp.int16)
        extra.append((scale, jnp.sum(jnp.where(eye, x, 0.0), axis=0, keepdims=True)))
    xpeer = {"plane": (p + 2) % planes}
    cpeer = {"plane": p + 1 - 2 * (p % 2)}
    px = (p + 2) % planes
    pc = p + 1 - 2 * (p % 2)
    pcx = (pc + 2) % planes
    stage1, stage2x, stage2c, stage3 = [], [], [], []
    for o in range(1, spans):
        s = (me + spans - o) % spans
        out = remote(inv16.at[p], modes_ref.at[p, me], sems, 0, o, span_to(o))
        out.start()
        stage1.append((out, remote(inv16.at[p], modes_ref.at[p, s], sems, 0, o, span_to(o))))
        stage2x.append((remote(modes_ref.at[p, s], modes_ref.at[p, s], sems, 1, o, xpeer),
                        remote(modes_ref.at[p, s], modes_ref.at[px, s], sems, 1, o, xpeer)))
        stage2c.append((remote(modes_ref.at[p, s], modes_ref.at[p, s], sems, 2, o, cpeer),
                        remote(modes_ref.at[p, s], modes_ref.at[pc, s], sems, 2, o, cpeer)))
        stage3.append((remote(modes_ref.at[px, s], modes_ref.at[px, s], sems, 3, o, cpeer),
                       remote(modes_ref.at[px, s], modes_ref.at[pcx, s], sems, 3, o, cpeer)))

    tail[...] = jnp.zeros_like(tail)
    for k in range(slabs):
        tail[k % spans, k // spans:k // spans + 1, :] = adj_ref[k // zdev, k % zdev, bulk:q, :]
    for t in range(NSTEP):
        slot = step_ref[t]
        for k in range(2 * zdev):
            row = ck_ref[slot, k // zdev, k % zdev].astype(F32)[bulk:q, :]
            tail[k, 2 + t:3 + t, :] = row
    for i in range(sets):
        parts = []
        for g in range(spans):
            h = spans * i + g
            k, r = h // 2, (h % 2) * half
            parts.append(adj_ref[k // zdev, k % zdev, r:r + half, :])
        parts = swap_blocks(parts, share)
        for d in range(spans):
            stage[d, i * half:(i + 1) * half, :] = parts[d]
    parts = swap_blocks([tail[g] for g in range(spans)], share)
    more = jnp.concatenate([a for a, _ in extra] + [b for _, b in extra], axis=0)
    for d in range(spans):
        snd[d], scales = coded_blocks(stage[d], sets, half)
        tsnd[d, :8] = jnp.concatenate([parts[d][:5]] + scales, axis=0)
        tsnd[d, 8:] = more
    tails = []
    fields, speeds = [], [[] for _ in range(NSTEP)]
    for o in range(1, spans):
        to, s = (me + o) % spans, (me + spans - o) % spans
        out = remote(snd.at[to], rcv.at[me], sems, 4, o, span_to(o))
        out.start()
        fields.append((out, remote(snd.at[to], rcv.at[s], sems, 4, o, span_to(o))))
        out = remote(tsnd.at[to], trc.at[me], sems, 13, o, span_to(o))
        out.start()
        tails.append((out, remote(tsnd.at[to], trc.at[s], sems, 13, o, span_to(o))))
    own = pltpu.make_async_copy(snd.at[me], rcv.at[me], local_sem.at[0])
    own.start()
    town = pltpu.make_async_copy(tsnd.at[me], trc.at[me], local_sem.at[2 + zdev])
    town.start()
    wide = zdev * LANES
    for t in range(NSTEP):
        slot = step_ref[t]
        parts = [ck_ref[slot, k // zdev, k % zdev].astype(F32)[:bulk] for k in range(2 * zdev)]
        parts = swap_blocks(parts, share)
        for d in range(spans):
            vsnd[d, t] = parts[d].astype(BF16)
        for o in range(1, spans):
            to, s = (me + o) % spans, (me + spans - o) % spans
            out = remote(vsnd.at[to, t], vrcv.at[me, t], sems, 5 + t, o, span_to(o))
            out.start()
            speeds[t].append((out, remote(vsnd.at[to, t], vrcv.at[s, t], sems, 5 + t, o, span_to(o))))
    vown = pltpu.make_async_copy(vsnd.at[me], vrcv.at[me], local_sem.at[1])
    vown.start()
    mine = [pltpu.make_async_copy(inv16.at[j], modes_ref.at[j, me], local_sem.at[2 + j])
            for j in range(zdev)]
    for c in mine:
        c.start()
    xs_ref[bulk:, :] = jnp.zeros_like(xs_ref[bulk:, :])
    vs_ref[:, :, bulk:, :] = jnp.zeros_like(vs_ref[:, :, bulk:, :])
    product[...] = jnp.zeros_like(product)
    lane = lax.broadcasted_iota(jnp.int32, (1, LANES), 1)
    rolled = pltpu.roll(metric_ref[...], (LANES - me * share) % LANES, 1)
    scale = jnp.where(lane < share, rolled, 0.0)
    k = share
    while k < LANES:
        scale = scale + pltpu.roll(scale, k, 1)
        k *= 2
    block = lax.broadcasted_iota(jnp.int32, (1, 3 * LANES), 1) % LANES // share
    gap = jnp.zeros((LANES - qp, 3 * LANES), BF16)
    first = jnp.concatenate([scale[0:1]] * zdev, axis=1)
    second = jnp.concatenate([scale[1:2]] * zdev, axis=1)

    for o in range(spans - 1):
        stage1[o][1].wait_recv()
        stage2x[o][0].start()
        stage2c[o][0].start()
    for o in range(spans - 1):
        stage2x[o][1].wait_recv()
        stage3[o][0].start()
    own.wait()
    town.wait()
    for c in fields + tails:
        c[1].wait_recv()
    for s in range(spans):
        x = rcv[s].astype(jnp.int32).astype(F32)
        for i in range(sets):
            stage[s, i * half:(i + 1) * half, :] = x[i * half:(i + 1) * half] * trc[s, 5 + i:6 + i, :]
    for i in range(sets):
        parts = swap_blocks([stage[s, i * half:(i + 1) * half, :] for s in range(spans)], share)
        for g in range(spans):
            h = spans * i + g
            k, r = h // 2, (h % 2) * half
            xs_ref[r:r + half, k * LANES:(k + 1) * LANES] = parts[g]
    parts = swap_blocks([trc[s, :8, :] for s in range(spans)], share)
    for k in range(slabs):
        xs_ref[bulk:q, k * LANES:(k + 1) * LANES] = parts[k % spans][k // spans:k // spans + 1]
    for t in range(NSTEP):
        for k in range(2 * zdev):
            z = k % zdev
            vs_ref[t, k // zdev, bulk:q, z * LANES:(z + 1) * LANES] = parts[k][2 + t:3 + t]
    vown.wait()

    for t in range(NSTEP):
        for c in speeds[t]:
            c[1].wait_recv()
        parts = swap_blocks([vrcv[s, t].astype(F32) for s in range(spans)], share)
        for k in range(2 * zdev):
            z = k % zdev
            vs_ref[t, k // zdev, :bulk, z * LANES:(z + 1) * LANES] = parts[k]
        v0 = vs_ref[t, 0] * first
        v1 = vs_ref[t, 1] * second
        for c in range(3):
            x = xs_ref[:, c * wide:(c + 1) * wide]
            high, low = split(x)
            d = dot(diff_ref[...], jnp.concatenate([high, low, high], axis=0))
            coef[c * qp:(c + 1) * qp, :] = x + v0 * d[:qp] + v1 * d[qp:]
        y = transform(coef[...], basis_ref, False)
        coef[...] = y
        if t == 0:
            for c in mine:
                c.wait()
            for group in (stage2c, stage3):
                for c in group:
                    c[1].wait_recv()
            for j in range(zdev):
                for s in range(spans):
                    x = decoded(modes_ref[j, s], trc[s, 8 + j:9 + j, :])
                    x = jnp.where(eye, trc[s, 8 + zdev + j:9 + zdev + j, :], x)
                    high, low = split(x)
                    modes_cat[j, s * qp:(s + 1) * qp, :LANES] = high
                    modes_cat[j, s * qp:(s + 1) * qp, LANES:2 * LANES] = high
                    modes_cat[j, s * qp:(s + 1) * qp, 2 * LANES:] = low
        for j in range(zdev):
            lanes = slice(j * LANES, (j + 1) * LANES)
            x = jnp.concatenate([coef[c * qp:(c + 1) * qp, lanes] for c in range(3)], axis=1)
            high, low = split(x)
            r = dot(modes_cat[j], jnp.concatenate([high, gap, low, gap, high, gap], axis=0))
            acc = r[:qp]
            for s in range(1, spans):
                acc = jnp.where(block == s, r[s * qp:(s + 1) * qp], acc)
            for c in range(3):
                solved[c * qp:(c + 1) * qp, lanes] = acc[:, c * LANES:(c + 1) * LANES]
        y = transform(solved[...], basis_ref, True)
        for c in range(3):
            xs_ref[:, c * wide:(c + 1) * wide] = y[c * qp:(c + 1) * qp]
        product[...] += y[qp:2 * qp] * vs_ref[t, 1]

    def exchange(kind, size, axis, pick_src, dst):
        at = lax.axis_index(axis)
        pairs = []
        for o in range(1, size):
            to, s = (at + o) % size, (at + size - o) % size
            out = remote(pick_src(to), dst.at[at], sems, kind, o, {axis: to})
            out.start()
            pairs.append((out, remote(pick_src(to), dst.at[s], sems, kind, o, {axis: to})))
        return pairs

    for k in range(slabs):
        tail[k % spans, k // spans:k // spans + 1, :] = xs_ref[bulk:q, k * LANES:(k + 1) * LANES]
    for i in range(sets):
        parts = []
        for g in range(spans):
            h = spans * i + g
            k, r = h // 2, (h % 2) * half
            parts.append(xs_ref[r:r + half, k * LANES:(k + 1) * LANES])
        parts = swap_blocks(parts, share)
        for d in range(spans):
            stage[d, i * half:(i + 1) * half, :] = parts[d]
    parts = swap_blocks([tail[g] for g in range(spans)], share)
    for d in range(spans):
        bsnd[d], scales = coded_blocks(stage[d], sets, half)
        tbsnd[d] = jnp.concatenate([parts[d][:5]] + scales, axis=0)
    returned = exchange(10, spans, "span", lambda to: bsnd.at[to], back)
    returned += exchange(14, spans, "span", lambda to: tbsnd.at[to], tback)
    tbown = pltpu.make_async_copy(tbsnd.at[me], tback.at[me], local_sem.at[2])
    tbown.start()
    bown = pltpu.make_async_copy(bsnd.at[me], back.at[me], local_sem.at[1])
    bown.start()
    high, low = split(product[...].T)
    left = jnp.concatenate([high, low], axis=1)
    pair = 2 * LANES
    base = p * LANES + me * share
    mode = lax.broadcasted_iota(jnp.int32, (qp, pair), 0)
    near = lax.broadcasted_iota(jnp.int32, (LANES, pair), 0) % share + base
    for piece in range(planes):
        lanes = slice(piece * pair, (piece + 1) * pair)
        got = 0.0
        for k in range(2):
            pick = jnp.where(local_ref[k:k + 1, lanes] == mode, 1.0, 0.0).astype(BF16)
            keep = jnp.where(elem_ref[k:k + 1, lanes] == near, 1.0, 0.0)
            keep = jnp.concatenate([keep] * zdev, axis=0)
            got = got + dot(left, jnp.concatenate([pick, pick], axis=0)) * keep
        acc = dot(place_ref[...], jnp.concatenate(split(got), axis=0))
        acc = acc[:, :LANES] + pltpu.roll(acc[:, LANES:], zdev, 0)
        for s in range(spans):
            wall[piece, s] = acc[s * 8:(s + 1) * 8]
    rows = exchange(8, planes, "plane", lambda to: wall.at[to], rows_in)
    rown = pltpu.make_async_copy(wall.at[p], rows_in.at[p], local_sem.at[0])
    rown.start()

    rown.wait()
    for c in rows:
        c[1].wait_recv()
    part[...] = sum(rows_in[s] for s in range(planes))
    walls = exchange(9, spans, "span", lambda to: part.at[to], wrcv)
    wown = pltpu.make_async_copy(part.at[me], wrcv.at[me], local_sem.at[0])
    wown.start()
    wown.wait()
    for c in walls:
        c[1].wait_recv()
    both = sum(wrcv[s] for s in range(spans))
    sums = jnp.concatenate([both[:zdev], both[zdev:]], axis=1)
    weight = weight_ref[:, pl.ds(pl.multiple_of(p * 2 * LANES, 2 * LANES), 2 * LANES)]
    weighted = weight * sums
    weighted_ref[...] = weighted
    sq = weighted * weighted
    square[...] = jnp.broadcast_to(jnp.sum(sq[:, :LANES] + sq[:, LANES:], axis=0, keepdims=True), (8, LANES))
    squares = exchange(11, spans, "span", lambda to: square, srcv)
    srcv[me] = square[...]
    for c in squares:
        c[1].wait_recv()
    total[...] = sum(srcv[s] for s in range(spans))
    totals = exchange(12, planes, "plane", lambda to: total, trcv)
    trcv[p] = total[...]
    for c in totals:
        c[1].wait_recv()
    bown.wait()
    tbown.wait()
    for c in returned:
        c[1].wait_recv()
    for group in (stage1, stage2x, stage2c, stage3, fields, tails, *speeds, rows, walls, returned, squares, totals):
        for c in group:
            c[0].wait_send()


def split(x):
    high = x.astype(BF16)
    return high, (x - high.astype(F32)).astype(BF16)


def dot(a, b, dims=((1,), (0,))):
    return lax.dot_general(a, b, (dims, ((), ())), preferred_element_type=F32)


def transform(x, basis_ref, back):
    high, low = split(x)
    left = jnp.concatenate([high, high, low], axis=1)
    parts = [basis_ref[0], basis_ref[1], basis_ref[0]]
    right = jnp.concatenate(parts, axis=1 if back else 0)
    return dot(left, right, ((1,), (1,)) if back else ((1,), (0,)))


def finish_kernel(spans, planes, zdev, q, count, back, tback, weighted_ref, trcv, out_ref, grad_ref, stage):
    share = LANES // spans
    bulk = q - 1
    half = bulk // 2
    slabs = 3 * zdev
    sets = 2 * slabs // spans
    full = jnp.sum(sum(trcv[s] for s in range(planes))[0:1], axis=1, keepdims=True)
    grad_ref[...] = weighted_ref[...] * lax.rsqrt(full / count + 1e-06)
    for s in range(spans):
        x = back[s].astype(jnp.int32).astype(F32)
        for i in range(sets):
            stage[s, i * half:(i + 1) * half, :] = x[i * half:(i + 1) * half] * tback[s, 5 + i:6 + i, :]
    for i in range(sets):
        parts = swap_blocks([stage[s, i * half:(i + 1) * half, :] for s in range(spans)], share)
        for g in range(spans):
            h = spans * i + g
            k, r = h // 2, (h % 2) * half
            out_ref[k // zdev, r:r + half, k % zdev, :] = parts[g]
    parts = swap_blocks([tback[s] for s in range(spans)], share)
    for k in range(slabs):
        out_ref[k // zdev, bulk:q, k % zdev, :] = parts[k % spans][k // spans:k // spans + 1]


def halves(table):
    high = table.astype(np.float32).astype(ml_dtypes.bfloat16)
    low = (table - high.astype(np.float64)).astype(np.float32).astype(ml_dtypes.bfloat16)
    return np.stack([high, low])


def tables(spans, zdev, q, qp):
    share = LANES // spans
    fourier = fourier_table(spans * zdev)
    order = np.array([s * zdev + z for z in range(zdev) for s in range(spans)])
    basis = np.kron(fourier[order][:, order].T, np.eye(share))
    side = P_SIZE + 1
    matrix = chebyshev_matrix(P_SIZE)
    diff = np.zeros((2 * qp, qp))
    diff[:q, :q] = np.kron(matrix, np.eye(side))
    diff[qp:qp + q, :q] = np.kron(np.eye(side), matrix)
    place = np.zeros((spans * 8, zdev * LANES), ml_dtypes.bfloat16)
    for s in range(spans):
        for z in range(zdev):
            at = z * LANES + s * share
            place[s * 8 + z, at:at + share] = 1.0
    high, low = halves(diff)
    diff = np.concatenate([high, high, low], axis=1)
    place = np.concatenate([place, place], axis=1)
    return halves(basis), diff, place


def vmem(n):
    return [pl.BlockSpec(memory_space=pltpu.VMEM)] * n


def kernels_on_device(spans, planes, adjoint, checkpoints, checkpoint_step, metric,
                      helmholtz_inverse, wall_element, wall_local, wall_weight):
    _, zdev, q, _ = adjoint.shape
    wall_count = wall_element.shape[0]
    qp = -(-q // 16) * 16
    bulk, wide = q - 1, zdev * LANES
    rows = 3 * zdev * bulk // spans
    inverse = helmholtz_inverse.transpose(1, 0, 2)
    shape = jax.ShapeDtypeStruct
    basis, diff, place = tables(spans, zdev, q, qp)
    back, tback, weighted, squares = pl.pallas_call(
        functools.partial(step_kernel, spans, planes, zdev, q, qp),
        out_shape=(shape((spans, rows, LANES), jnp.int16), shape((spans, 8, LANES), F32),
                   shape((zdev, wall_count // planes), F32),
                   shape((planes, 8, LANES), F32)),
        in_specs=[pl.BlockSpec(memory_space=pltpu.SMEM)] + vmem(10),
        out_specs=tuple(vmem(4)),
        scratch_shapes=[
            pltpu.VMEM((qp, 3 * wide), F32),
            pltpu.VMEM((NSTEP, 2, qp, wide), F32),
            pltpu.VMEM((qp, LANES), F32),
            pltpu.VMEM((zdev, qp, LANES), jnp.int16),
            pltpu.VMEM((zdev, spans, qp, LANES), jnp.int16),
            pltpu.VMEM((spans, 8, LANES), F32),
            pltpu.VMEM((spans, rows, LANES), F32),
            pltpu.VMEM((spans, rows, LANES), jnp.int16),
            pltpu.VMEM((spans, 8 + 2 * zdev, LANES), F32),
            pltpu.VMEM((spans, rows, LANES), jnp.int16),
            pltpu.VMEM((spans, 8 + 2 * zdev, LANES), F32),
            pltpu.VMEM((spans, NSTEP, bulk, LANES), BF16),
            pltpu.VMEM((spans, NSTEP, bulk, LANES), BF16),
            pltpu.VMEM((3 * qp, wide), F32),
            pltpu.VMEM((3 * qp, wide), F32),
            pltpu.VMEM((qp, wide), F32),
            pltpu.VMEM((zdev, spans * qp, 3 * LANES), BF16),
            pltpu.VMEM((spans, rows, LANES), jnp.int16),
            pltpu.VMEM((spans, 8, LANES), F32),
            pltpu.VMEM((planes, spans, 8, LANES), F32),
            pltpu.VMEM((planes, spans, 8, LANES), F32),
            pltpu.VMEM((spans, 8, LANES), F32),
            pltpu.VMEM((spans, 8, LANES), F32),
            pltpu.VMEM((8, LANES), F32),
            pltpu.VMEM((spans, 8, LANES), F32),
            pltpu.VMEM((8, LANES), F32),
            pltpu.SemaphoreType.DMA((2, 15, spans)),
            pltpu.SemaphoreType.DMA((3 + zdev,)),
        ],
        compiler_params=pltpu.CompilerParams(collective_id=0, has_side_effects=True),
        name="steps",
    )(checkpoint_step, adjoint, checkpoints, inverse, metric, wall_element.T, wall_local.T,
      wall_weight, basis, diff, place)
    field, gradient = pl.pallas_call(
        functools.partial(finish_kernel, spans, planes, zdev, q, float(spans * zdev * wall_count)),
        out_shape=(shape((3, q, zdev, LANES), F32), shape((zdev, wall_count // planes), F32)),
        in_specs=vmem(4),
        out_specs=tuple(vmem(2)),
        scratch_shapes=[pltpu.VMEM((spans, rows, LANES), F32)],
        name="finish",
    )(back, tback, weighted, squares)
    return field.transpose(0, 2, 1, 3), gradient


def chosen(spans, planes, *args):
    zdev, q, elems = args[0].shape[1:]
    walls = args[5].shape[0]
    fits = (
        elems == LANES and spans == 2 * zdev and planes == zdev == 4
        and walls == planes * 2 * LANES and q % 16 == 1 and q < LANES
    )
    if fits:
        return kernels_on_device(spans, planes, *args)
    return on_device(*args)


def solution(mesh):
    placed = (
        P(None, "span", None, "plane"),
        P(None, None, "span", None, "plane"),
        P(),
        P(None, "plane"),
        P("span", None, None),
        P(),
        P(),
        P("span", None),
    )
    return jax.shard_map(
        functools.partial(chosen, mesh.shape["span"], mesh.shape["plane"]),
        mesh=mesh,
        in_specs=placed,
        out_specs=(P(None, "span", None, "plane"), P("span", "plane")),
        check_vma=False,
    )
```

profile of v0, /device:TPU:0, one launch (start us, length us, event | category | flops | bytes accessed | tf_op | source)
XLA Modules:
  0.0 63.9 jit_solution(4179950597995847540)
XLA Ops:
  0.6 1.9 %copy.13.adj_ref = f32[3,4,81,128]{3,2,1,0:T(8,128)} copy(f32[3,4,81,128]{3,1,2,0:T(4,128)} %param.11) | data formatting | bytes 995328 | tf_op args[0]
  2.5 2.7 %copy.14.ck_ref = bf16[8,2,4,81,128]{4,3,2,1,0:T(8,128)(2,1)} copy(bf16[8,2,4,81,128]{4,2,3,1,0:T(4,128)(2,1)} %param.12) | data formatting | bytes 2654208 | tf_op args[1]
  5.2 56.1 %steps.1 = (s16[8,120,128]{2,1,0:T(8,128)(2,1)}, f32[8,8,128]{2,1,0:T(8,128)}, f32[4,256]{1,0:T(4,128)}, f32[4,8,128]{2,1,0:T(8,128)}) custom-call(s32[3]{0:T(128)} %step_ref.1, f32[3,4,81,128]{3,2,1,0:T(8,128)} %copy.13.adj_ref, bf16[8,2,4,81,128]{4,3,2,1,0:T(8,128)(2,1)} %copy.14.ck_ref, f32[81,4,81]{2,1,0:T(4,128)} %bitcast.4, f32[2,128]{1,0:T(2,128)} %metric_ref.1, ...), custom_call_target="tpu_custom_call" | custom-call | tf_op jit(solution)/shard_map/steps/pallas_call | solution.py:547
  61.3 2.6 %finish.1 = (f32[3,81,4,128]{3,2,1,0:T(4,128)}, f32[4,256]{1,0:T(4,128)}) custom-call(s16[8,120,128]{2,1,0:T(8,128)(2,1)} %get-tuple-element.8.back, f32[8,8,128]{2,1,0:T(8,128)} %get-tuple-element.9.tback, f32[4,256]{1,0:T(4,128)} %get-tuple-element.10.weighted_ref, f32[4,8,128]{2,1,0:T(8,128)} %get-tuple-element.11.trcv), custom_call_target="tpu_custom_call" | custom-call | tf_op jit(solution)/shard_map/finish/pallas_call | solution.py:588
where the time goes:
time: 64.1 us; the launch traced here: 63.9 us
  Pallas kernels  58.7 us (92%)
  local copies, waits for them, and re-layouts  4.56 us (7%)
    pallas_call x1, Pallas kernels, kernels_on_device(): pl.pallas_call(functools.partial(step_kernel, spans, planes, zdev, q, qp)...  56.1 us
    unnamed x2, local copies, waits for them, and re-layouts  4.56 us
    pallas_call x1, Pallas kernels, kernels_on_device(): pl.pallas_call(functools.partial(finish_kernel, spans, planes, zdev, q, f...  2.58 us

commit v1 on v0

v1 whole, which is shorter than its diff:
```python
import functools

import jax
import jax.numpy as jnp
import ml_dtypes
import numpy as np
from jax import lax
from jax.experimental import pallas as pl
from jax.experimental.pallas import tpu as pltpu
from jax.sharding import PartitionSpec as P

P_SIZE = 8
NSTEP = 3


HIGHEST = lax.Precision.HIGHEST


def chebyshev_matrix(degree):
    points = np.arange(degree + 1)
    abscissa = np.cos(np.pi * points / degree)
    signed = np.where((points == 0) | (points == degree), 2.0, 1.0) * (-1.0) ** points
    spacing = abscissa[:, None] - abscissa[None, :] + np.eye(degree + 1)
    matrix = signed[:, None] / signed[None, :] / spacing
    return matrix - np.eye(degree + 1) * np.sum(matrix, axis=1)[:, None]


def fourier_table(length):
    row_index = np.arange(length)[:, None]
    column = np.arange(length)[None, :]
    wavenumber = (row_index + 1) // 2
    phase_angle = 2.0 * np.pi * wavenumber * column / length
    parity = row_index % 2
    base_rows = np.where(
        row_index == 0, 1.0, np.where(parity == 1, np.cos(phase_angle), np.sin(phase_angle))
    )
    row_scale = np.where(
        (row_index == 0) | (row_index == length - 1), 1.0 / np.sqrt(length), np.sqrt(2.0 / length)
    )
    return base_rows * row_scale


def transport(field_data, velocity, metric):
    side_nodes = P_SIZE + 1
    matrix = jnp.asarray(chebyshev_matrix(P_SIZE), jnp.float32)
    shaped = field_data.reshape(
        field_data.shape[0], field_data.shape[1], side_nodes, side_nodes, field_data.shape[3]
    )
    first_dir = jnp.einsum("ai,czibe->czabe", matrix, shaped, precision=HIGHEST).reshape(
        field_data.shape
    )
    second_dir = jnp.einsum("bi,czaie->czabe", matrix, shaped, precision=HIGHEST).reshape(
        field_data.shape
    )
    speed_data = velocity.astype(jnp.float32)
    return (
        field_data
        + speed_data[0] * (metric[0] * first_dir)
        + speed_data[1] * (metric[1] * second_dir)
    )


def forward_modes(gathered):
    basis_table = jnp.asarray(fourier_table(gathered.shape[1]), jnp.float32)
    return jnp.einsum("jz,czqe->cjqe", basis_table, gathered, precision=HIGHEST)


def backward_planes(solved):
    basis_table = jnp.asarray(fourier_table(solved.shape[1]), jnp.float32)
    return jnp.einsum("jz,cjqe->czqe", basis_table, solved, precision=HIGHEST)


def solve_modes(inverse_block, coefficients):
    return jnp.einsum("jqr,cjre->cjqe", inverse_block, coefficients, precision=HIGHEST)


def to_plane_layout(point_data):
    return lax.all_to_all(point_data, "span", split_axis=1, concat_axis=3, tiled=True)


def wall_terms(field_one, speed_one, flat_index, inside, wall_count):
    rows = field_one.shape[0]
    values = jnp.take(field_one.reshape(rows, -1), flat_index, axis=1)
    speeds = jnp.take(speed_one.reshape(rows, -1), flat_index, axis=1).astype(jnp.float32)
    product = jnp.where(inside, values * speeds, 0.0).reshape(rows, wall_count, 2)
    return jnp.sum(product, axis=2)


def on_device(
    adjoint,
    checkpoints,
    checkpoint_step,
    metric,
    helmholtz_inverse,
    wall_element,
    wall_local,
    wall_weight,
):
    planes_dev = adjoint.shape[1]
    elems_dev = adjoint.shape[3]
    wall_count = wall_element.shape[0]
    span_count = lax.axis_size("span")
    share = elems_dev // span_count
    all_modes = lax.all_gather(helmholtz_inverse, "span", axis=0, tiled=True)
    offset = lax.axis_index("plane") * elems_dev
    local_element = wall_element - offset
    inside = ((local_element >= 0) & (local_element < elems_dev)).reshape(-1)
    flat_index = (wall_local * elems_dev + jnp.clip(local_element, 0, elems_dev - 1)).reshape(-1)
    velocity = jnp.stack([
        lax.dynamic_index_in_dim(checkpoints, checkpoint_step[s], 0, keepdims=False)
        for s in range(NSTEP)
    ])
    velocity = lax.all_to_all(velocity, "span", split_axis=4, concat_axis=2, tiled=True)
    field = lax.all_to_all(adjoint, "span", split_axis=3, concat_axis=1, tiled=True)
    scale = lax.dynamic_slice_in_dim(metric, lax.axis_index("span") * share, share, 1)
    product = 0.0
    for substep in range(NSTEP):
        advected = transport(field, velocity[substep], scale)
        field = backward_planes(solve_modes(all_modes, forward_modes(advected)))
        product = product + field[1] * velocity[substep, 1].astype(jnp.float32)
    both = to_plane_layout(jnp.concatenate([field, product[None]], axis=0))
    gathered = jnp.take(both[3].reshape(planes_dev, -1), flat_index, axis=1)
    partial_sum = jnp.where(inside, gathered, 0.0).reshape(planes_dev, wall_count, 2).sum(axis=2)
    weighted = wall_weight * partial_sum
    grad_share = lax.psum_scatter(weighted, "plane", scatter_dimension=1, tiled=True)
    square_total = lax.psum(jnp.sum(grad_share * grad_share), ("span", "plane"))
    inverse_rms = lax.rsqrt(square_total / (planes_dev * span_count * wall_count) + 1e-06)
    return (both[:3], grad_share * inverse_rms)


MESH = pl.DeviceIdType.MESH
F32 = jnp.float32
BF16 = jnp.bfloat16
LANES = 128


def swap_blocks(parts, share):
    count = len(parts)
    width = count * share
    lane = lax.broadcasted_iota(jnp.int32, parts[0].shape, 1)
    k = count // 2
    while k:
        upper = (lane // (k * share)) % 2 == 1
        new = list(parts)
        for i in range(count):
            if (i // k) % 2 == 0:
                a, b = parts[i], parts[i + k]
                new[i] = jnp.where(upper, pltpu.roll(b, k * share, 1), a)
                new[i + k] = jnp.where(upper, b, pltpu.roll(a, width - k * share, 1))
        parts = new
        k //= 2
    return parts


def coded(x):
    top = jnp.maximum(jnp.max(jnp.abs(x), axis=0, keepdims=True), 1e-30)
    return jnp.round(x * (32767.0 / top)).astype(jnp.int32), top * (1.0 / 32767.0)


def remote(src, dst, sem_out, sem_in, target):
    return pltpu.make_async_remote_copy(
        src_ref=src, dst_ref=dst, send_sem=sem_out, recv_sem=sem_in,
        device_id=target, device_id_type=MESH,
    )


def mode_block(x, eye, q):
    diag = jnp.sum(jnp.where(eye, x, 0.0), axis=0, keepdims=True)
    off = jnp.where(eye, 0.0, x)
    row = lax.broadcasted_iota(jnp.int32, x.shape, 0)
    power = power_of(jnp.max(jnp.abs(off), axis=0, keepdims=True))
    power_d = power_of(jnp.abs(diag))
    unit = diag * (32767.0 * jnp.exp2(-power_d))
    high = jnp.round(unit)
    low = jnp.round((unit - high) * 32767.0)
    whole = jnp.round(off * (32767.0 * jnp.exp2(-power)))
    for i, extra in enumerate((power, power_d, high, low)):
        whole = jnp.where(row == q + i, extra, whole)
    return whole.astype(jnp.int32).astype(jnp.int16)


def power_of(top):
    return jnp.ceil(jnp.log2(jnp.maximum(top, 1e-30)))


def mode_matrix(block, eye, q):
    x = block.astype(jnp.int32).astype(F32)
    scale = jnp.exp2(x[q:q + 1]) * (1.0 / 32767.0)
    diag = (x[q + 2:q + 3] + x[q + 3:q + 4] * (1.0 / 32767.0)) * (jnp.exp2(x[q + 1:q + 2]) * (1.0 / 32767.0))
    row = lax.broadcasted_iota(jnp.int32, x.shape, 0)
    return jnp.where(eye, diag, jnp.where(row < q, x, 0.0) * scale)


def step_kernel(spans, planes, zdev, q, qp,
                step_h, adj_h, ck_h, inv_h, metric_h, elem_h, local_h, weight_h, basis_h, diff_h, place_h,
                back, tback, weighted_ref, srcv,
                step_ref, adj_ref, ck_ref, inv_ref, metric_ref, elem_ref, local_ref, weight_ref,
                basis_ref, diff_ref, place_ref,
                home, vhome, vf, xs_ref, vs_ref, v0_ref, padded, inv16, modes_ref, tail,
                snd, tsnd, rcv, trc, vsnd, vrcv, wsnd, wrc,
                coef, solved, product, kept, modes_cat, bsnd, tbsnd,
                picks, keeps, wall, rows_in, part, wrcv, square, sems, sqsems, load_sem, local_sem):
    share = LANES // spans
    me, p = lax.axis_index("span"), lax.axis_index("plane")
    bulk = q - 1
    half = bulk // 2
    slabs = 3 * zdev
    wide = zdev * LANES

    barrier = pltpu.get_barrier_semaphore()
    for a in range(planes):
        for o in range(spans):
            if a or o:
                pl.semaphore_signal(
                    barrier, 1, device_id={"plane": (p + a) % planes, "span": (me + o) % spans},
                    device_id_type=MESH)
    names = ("inv", "step", "metric", "adj", "ck", "diff", "elem", "local", "place", "basis", "weight")
    pairs = ((inv_h, inv_ref), (step_h, step_ref), (metric_h, metric_ref), (adj_h, adj_ref), (ck_h, ck_ref),
             (diff_h, diff_ref), (elem_h, elem_ref), (local_h, local_ref), (place_h, place_ref),
             (basis_h, basis_ref), (weight_h, weight_ref))
    loads = {}
    for i, (src, dst) in enumerate(pairs):
        loads[names[i]] = pltpu.make_async_copy(src, dst, load_sem.at[i])
        loads[names[i]].start()

    def span_to(o):
        return {"span": (me + o) % spans}

    def sem(kind, o):
        return sems.at[0, kind, o], sems.at[1, kind, o]

    started = []

    def send(src, dst, kind, o, target):
        out = remote(src, dst, *sem(kind, o), target)
        out.start()
        started.append(out)

    def to_peers(kind, src, dst):
        incoming = []
        for o in range(1, spans):
            to, s = (me + o) % spans, (me + spans - o) % spans
            send(src(to), dst(me), kind, o, span_to(o))
            incoming.append(remote(src(to), dst(s), *sem(kind, o), span_to(o)))
        return incoming

    padded[...] = jnp.zeros_like(padded)
    tail[...] = jnp.zeros_like(tail)
    home[bulk:, :] = jnp.zeros_like(home[bulk:, :])
    vhome[:, bulk:, :] = jnp.zeros_like(vhome[:, bulk:, :])
    xs_ref[bulk:, :] = jnp.zeros_like(xs_ref[bulk:, :])
    vs_ref[:, :, bulk:, :] = jnp.zeros_like(vs_ref[:, :, bulk:, :])
    v0_ref[bulk:, :] = jnp.zeros_like(v0_ref[bulk:, :])
    eye = (lax.broadcasted_iota(jnp.int32, (qp, LANES), 0)
           == lax.broadcasted_iota(jnp.int32, (qp, LANES), 1))

    loads["inv"].wait()
    for j in range(zdev):
        padded[:q, :q] = inv_ref[:, j, :]
        inv16[j] = mode_block(padded[...], eye, q)

    for name in ("step", "metric", "adj", "ck", "diff"):
        loads[name].wait()
    for t in range(NSTEP):
        slot = step_ref[t]
        for k in range(2):
            vf[t, k] = ck_ref[slot, k].astype(F32)
    for k in range(2):
        for z in range(zdev):
            vhome[k, :q, z * LANES:(z + 1) * LANES] = vf[0, k, :, z, :]
    for k in range(slabs):
        home[:q, k * LANES:(k + 1) * LANES] = adj_ref[k // zdev, :, k % zdev, :]
    here = metric_ref[...]
    first = jnp.concatenate([here[0:1]] * zdev, axis=1)
    second = jnp.concatenate([here[1:2]] * zdev, axis=1)
    v0 = vhome[0] * first
    v1 = vhome[1] * second
    scales = [None] * 3
    for c in (1, 0, 2):
        lanes = slice(c * wide, (c + 1) * wide)
        moved = transport_block(home[:, lanes], v0, v1, diff_ref, qp)
        home[:, lanes] = moved
        scales[c] = coded_component(moved, snd, c, spans, share, half)
    for k in range(slabs):
        tail[k % spans, k // spans:k // spans + 1, :] = home[bulk:q, k * LANES:(k + 1) * LANES]
    for k in range(2 * zdev):
        for t in range(1, NSTEP):
            tail[k, 1 + t:2 + t, :] = vf[t, k // zdev, bulk:q, k % zdev, :]
    for z in range(zdev):
        tail[z, 1 + NSTEP:2 + NSTEP, :] = vf[0, 1, bulk:q, z, :]
    parts = swap_blocks([tail[g] for g in range(spans)], share)
    for d in range(spans):
        tsnd[d] = jnp.concatenate([parts[d][:5]] + [scales[c][d] for c in range(3)], axis=0)

    pl.semaphore_wait(barrier, spans * planes - 1)

    xpeer = {"plane": (p + 2) % planes}
    cpeer = {"plane": p + 1 - 2 * (p % 2)}
    px = (p + 2) % planes
    pc = p + 1 - 2 * (p % 2)
    pcx = (pc + 2) % planes
    mate = me + 1 - 2 * (me % 2)
    to_mate = {"span": mate}

    def block_of(i):
        return (me + spans - i) % spans if i % 2 == 0 else (mate + spans - i + 1) % spans

    mode_in = {}
    for i in range(2, spans, 2):
        send(inv16.at[p], modes_ref.at[p, me], 0, i, span_to(i))
        mode_in[i] = remote(inv16.at[p], modes_ref.at[p, block_of(i)], *sem(0, i), span_to(i))
    send(inv16.at[p], modes_ref.at[p, me], 0, 1, to_mate)
    mode_in[1] = remote(inv16.at[p], modes_ref.at[p, mate], *sem(0, 1), to_mate)
    for i in range(2, spans, 2):
        s = block_of(i + 1)
        mode_in[i + 1] = remote(modes_ref.at[p, s], modes_ref.at[p, s], *sem(0, i + 1), to_mate)
    fields = [None] * 3
    for c in (1, 0):
        fields[c] = to_peers(4 + c, lambda to: snd.at[c, to], lambda s: rcv.at[c, s])
    tails = to_peers(7, lambda to: tsnd.at[to], lambda s: trc.at[s])
    own = []
    for c in range(3):
        own.append(pltpu.make_async_copy(snd.at[c, me], rcv.at[c, me], local_sem.at[c]))
    own.append(pltpu.make_async_copy(tsnd.at[me], trc.at[me], local_sem.at[3]))
    own += [pltpu.make_async_copy(inv16.at[j], modes_ref.at[j, me], local_sem.at[4 + j]) for j in range(zdev)]
    for c in own:
        c.start()

    speeds = [None] * NSTEP
    for t in range(1, NSTEP):
        parts = swap_blocks([vf[t, k // zdev, :bulk, k % zdev, :] for k in range(2 * zdev)], share)
        for d in range(spans):
            vsnd[t - 1, d] = parts[d].astype(BF16)
        speeds[t] = to_peers(7 + t, lambda to: vsnd.at[t - 1, to], lambda s: vrcv.at[t - 1, s])
    parts = []
    for g in range(spans):
        r = (g % 2) * half
        parts.append(vf[0, 1, r:r + half, g // 2, :])
    parts = swap_blocks(parts, share)
    for d in range(spans):
        wsnd[d] = parts[d].astype(BF16)
    speeds[0] = to_peers(10, lambda to: wsnd.at[to], lambda s: wrc.at[s])
    fields[2] = to_peers(6, lambda to: snd.at[2, to], lambda s: rcv.at[2, s])
    vown = [pltpu.make_async_copy(vsnd.at[t, me], vrcv.at[t, me], local_sem.at[4 + zdev + t]) for t in range(NSTEP - 1)]
    vown.append(pltpu.make_async_copy(wsnd.at[me], wrc.at[me], local_sem.at[3 + zdev + NSTEP]))
    for c in vown:
        c.start()

    later = []
    for i in [2, 1, 4, 6, 3, 5, 7]:
        mode_in[i].wait_recv()
        s = block_of(i)
        if i % 2 == 0:
            send(modes_ref.at[p, s], modes_ref.at[p, s], 0, i + 1, to_mate)
        send(modes_ref.at[p, s], modes_ref.at[p, s], 1, i, xpeer)
        send(modes_ref.at[p, s], modes_ref.at[p, s], 2, i, cpeer)
        later.append((i, s))

    lane = lax.broadcasted_iota(jnp.int32, (1, LANES), 1)
    rolled = pltpu.roll(metric_ref[...], (LANES - me * share) % LANES, 1)
    scale = jnp.where(lane < share, rolled, 0.0)
    k = share
    while k < LANES:
        scale = scale + pltpu.roll(scale, k, 1)
        k *= 2
    first = jnp.concatenate([scale[0:1]] * zdev, axis=1)
    second = jnp.concatenate([scale[1:2]] * zdev, axis=1)
    loads["elem"].wait()
    loads["local"].wait()
    pair = 2 * LANES
    base = p * LANES + me * share
    mode = lax.broadcasted_iota(jnp.int32, (qp, pair), 0)
    near = lax.broadcasted_iota(jnp.int32, (LANES, pair), 0) % share + base
    for piece in range(planes):
        lanes = slice(piece * pair, (piece + 1) * pair)
        for k in range(2):
            pick = jnp.where(local_ref[k:k + 1, lanes] == mode, 1.0, 0.0).astype(BF16)
            picks[piece, k] = jnp.concatenate([pick, pick], axis=0)
            keeps[piece, k] = jnp.where(elem_ref[k:k + 1, lanes] == near, 1.0, 0.0)
    for name in ("basis", "place", "weight"):
        loads[name].wait()

    across, beside, corner = [], [], []
    for i, s in later:
        remote(modes_ref.at[p, s], modes_ref.at[px, s], *sem(1, i), xpeer).wait_recv()
        send(modes_ref.at[px, s], modes_ref.at[px, s], 3, i, cpeer)
        beside.append(remote(modes_ref.at[p, s], modes_ref.at[pc, s], *sem(2, i), cpeer))
        corner.append(remote(modes_ref.at[px, s], modes_ref.at[pcx, s], *sem(3, i), cpeer))

    for c in own:
        c.wait()
    for c in fields[1] + fields[0] + tails:
        c.wait_recv()

    def unpack(c):
        parts = [rcv[c, s].astype(jnp.int32).astype(F32) * trc[s, 5 + c:6 + c, :] for s in range(spans)]
        parts = swap_blocks(parts, share)
        for g in range(spans):
            k, r = c * zdev + g // 2, (g % 2) * half
            xs_ref[r:r + half, k * LANES:(k + 1) * LANES] = parts[g]

    parts = swap_blocks([trc[s] for s in range(spans)], share)
    for k in range(slabs):
        xs_ref[bulk:q, k * LANES:(k + 1) * LANES] = parts[k % spans][k // spans:k // spans + 1]
    for k in range(2 * zdev):
        z = k % zdev
        for t in range(1, NSTEP):
            vs_ref[t - 1, k // zdev, bulk:q, z * LANES:(z + 1) * LANES] = parts[k][1 + t:2 + t]
    for z in range(zdev):
        v0_ref[bulk:q, z * LANES:(z + 1) * LANES] = parts[z][1 + NSTEP:2 + NSTEP]
    unpack(0)
    unpack(1)

    for c in beside + corner:
        c.wait_recv()
    for j in range(zdev):
        for s in range(spans):
            high, low = split(mode_matrix(modes_ref[j, s], eye, q))
            modes_cat[j, s * qp:(s + 1) * qp, :LANES] = high
            modes_cat[j, s * qp:(s + 1) * qp, LANES:2 * LANES] = high
            modes_cat[j, s * qp:(s + 1) * qp, 2 * LANES:] = low

    def step(group, t):
        count = len(group)
        rows = slice(group[0] * qp, (group[-1] + 1) * qp)
        if t:
            v0 = vs_ref[t - 1, 0] * first
            v1 = vs_ref[t - 1, 1] * second
        for c in group:
            x = xs_ref[:, c * wide:(c + 1) * wide]
            if t:
                x = transport_block(x, v0, v1, diff_ref, qp)
            coef[c * qp:(c + 1) * qp, :] = x
        coef[rows, :] = transform(coef[rows, :], basis_ref, False)
        block = lax.broadcasted_iota(jnp.int32, (1, count * LANES), 1) % LANES // share
        gap = jnp.zeros((LANES - qp, count * LANES), BF16)
        for j in range(zdev):
            lanes = slice(j * LANES, (j + 1) * LANES)
            x = jnp.concatenate([coef[c * qp:(c + 1) * qp, lanes] for c in group], axis=1)
            high, low = split(x)
            r = dot(modes_cat[j], jnp.concatenate([high, gap, low, gap, high, gap], axis=0))
            acc = r[:qp]
            for s in range(1, spans):
                acc = jnp.where(block == s, r[s * qp:(s + 1) * qp], acc)
            for i, c in enumerate(group):
                solved[c * qp:(c + 1) * qp, lanes] = acc[:, i * LANES:(i + 1) * LANES]
        y = transform(solved[rows, :], basis_ref, True)
        for i, c in enumerate(group):
            xs_ref[:, c * wide:(c + 1) * wide] = y[i * qp:(i + 1) * qp]

    def unpack_speed(t):
        for c in speeds[t]:
            c.wait_recv()
        parts = swap_blocks([vrcv[t - 1, s].astype(F32) for s in range(spans)], share)
        for k in range(2 * zdev):
            z = k % zdev
            vs_ref[t - 1, k // zdev, :bulk, z * LANES:(z + 1) * LANES] = parts[k]

    one = slice(wide, 2 * wide)

    step((0, 1), 0)
    kept[...] = xs_ref[:, one]

    for c in vown:
        c.wait()
    unpack_speed(1)

    step((0, 1), 1)
    product[...] = xs_ref[:, one] * vs_ref[0, 1]

    unpack_speed(2)

    step((0, 1), 2)

    for c in speeds[0]:
        c.wait_recv()
    parts = swap_blocks([wrc[s].astype(F32) for s in range(spans)], share)
    for g in range(spans):
        z, r = g // 2, (g % 2) * half
        v0_ref[r:r + half, z * LANES:(z + 1) * LANES] = parts[g]
    product[...] += kept[...] * v0_ref[...] + xs_ref[:, one] * vs_ref[1, 1]

    high, low = split(product[...].T)
    left = jnp.concatenate([high, low], axis=1)
    for piece in range(planes):
        got = 0.0
        for k in range(2):
            keep = jnp.concatenate([keeps[piece, k]] * zdev, axis=0)
            got = got + dot(left, picks[piece, k]) * keep
        acc = dot(place_ref[...], jnp.concatenate(split(got), axis=0))
        acc = acc[:, :LANES] + pltpu.roll(acc[:, LANES:], zdev, 0)
        for s in range(spans):
            wall[piece, s] = acc[s * 8:(s + 1) * 8]
    rows = []
    for o in range(1, planes):
        to, s = (p + o) % planes, (p + planes - o) % planes
        send(wall.at[to], rows_in.at[p], 11, o, {"plane": to})
        rows.append(remote(wall.at[to], rows_in.at[s], *sem(11, o), {"plane": to}))
    rown = pltpu.make_async_copy(wall.at[p], rows_in.at[p], local_sem.at[0])
    rown.start()

    scales = [None] * 3
    returned = []
    for c in (0, 1):
        scales[c] = coded_component(xs_ref[:, c * wide:(c + 1) * wide], bsnd, c, spans, share, half)
    rown.wait()
    for c in rows:
        c.wait_recv()
    part[...] = sum(rows_in[s] for s in range(planes))
    walls = to_peers(12, lambda to: part.at[to], lambda s: wrcv.at[s])
    wown = pltpu.make_async_copy(part.at[me], wrcv.at[me], local_sem.at[0])
    wown.start()
    for c in (0, 1):
        returned += to_peers(13 + c, lambda to: bsnd.at[c, to], lambda s: back.at[c, s])

    for c in fields[2]:
        c.wait_recv()
    unpack(2)

    step((2,), 0)
    wown.wait()
    for c in walls:
        c.wait_recv()
    both = sum(wrcv[s] for s in range(spans))
    sums = jnp.concatenate([both[:zdev], both[zdev:]], axis=1)
    weight = weight_ref[:, pl.ds(pl.multiple_of(p * 2 * LANES, 2 * LANES), 2 * LANES)]
    weighted = weight * sums
    weighted_ref[...] = weighted
    sq = weighted * weighted
    square[...] = jnp.sum(sq[:, :LANES] + sq[:, LANES:], axis=0, keepdims=True)
    squares = []
    for a in range(planes):
        for o in range(spans):
            if a or o:
                to = {"plane": (p + a) % planes, "span": (me + o) % spans}
                n = a * spans + o
                out = remote(square, srcv.at[p, me], sqsems.at[0, n], sqsems.at[1, n], to)
                out.start()
                started.append(out)
                squares.append(remote(
                    square, srcv.at[(p + planes - a) % planes, (me + spans - o) % spans],
                    sqsems.at[0, n], sqsems.at[1, n], to))
    srcv[p, me] = square[...]

    step((2,), 1)
    step((2,), 2)

    scales[2] = coded_component(xs_ref[:, 2 * wide:], bsnd, 2, spans, share, half)
    for k in range(slabs):
        tail[k % spans, k // spans:k // spans + 1, :] = xs_ref[bulk:q, k * LANES:(k + 1) * LANES]
    parts = swap_blocks([tail[g] for g in range(spans)], share)
    for d in range(spans):
        tbsnd[d] = jnp.concatenate([parts[d][:5]] + [scales[c][d] for c in range(3)], axis=0)
    returned += to_peers(15, lambda to: bsnd.at[2, to], lambda s: back.at[2, s])
    returned += to_peers(16, lambda to: tbsnd.at[to], lambda s: tback.at[s])
    bown = [pltpu.make_async_copy(bsnd.at[c, me], back.at[c, me], local_sem.at[c]) for c in range(3)]
    bown.append(pltpu.make_async_copy(tbsnd.at[me], tback.at[me], local_sem.at[3]))
    for c in bown:
        c.start()

    for c in squares:
        c.wait_recv()
    for c in bown:
        c.wait()
    for c in returned:
        c.wait_recv()
    for c in started:
        c.wait_send()


def transport_block(x, v0, v1, diff_ref, qp):
    high, low = split(x)
    d = dot(diff_ref[...], jnp.concatenate([high, low, high], axis=0))
    return x + v0 * d[:qp] + v1 * d[qp:]


def coded_component(x, out, c, spans, share, half):
    parts = []
    for g in range(spans):
        z, r = g // 2, (g % 2) * half
        parts.append(x[r:r + half, z * LANES:(z + 1) * LANES])
    parts = swap_blocks(parts, share)
    scales = []
    for d in range(spans):
        whole, scale = coded(parts[d])
        out[c, d] = whole.astype(jnp.int16)
        scales.append(scale)
    return scales


def split(x):
    high = x.astype(BF16)
    return high, (x - high.astype(F32)).astype(BF16)


def dot(a, b, dims=((1,), (0,))):
    return lax.dot_general(a, b, (dims, ((), ())), preferred_element_type=F32)


def transform(x, basis_ref, back):
    high, low = split(x)
    left = jnp.concatenate([high, high, low], axis=1)
    parts = [basis_ref[0], basis_ref[1], basis_ref[0]]
    right = jnp.concatenate(parts, axis=1 if back else 0)
    return dot(left, right, ((1,), (1,)) if back else ((1,), (0,)))


def finish_kernel(spans, planes, zdev, q, count, back, tback, weighted_ref, srcv, out_ref, grad_ref):
    share = LANES // spans
    bulk = q - 1
    half = bulk // 2
    slabs = 3 * zdev
    squares = sum(srcv[a, s] for a in range(planes) for s in range(spans))
    full = jnp.sum(squares, axis=1, keepdims=True)
    grad_ref[...] = weighted_ref[...] * lax.rsqrt(full / count + 1e-06)
    for c in range(3):
        parts = [back[c, s].astype(jnp.int32).astype(F32) * tback[s, 5 + c:6 + c, :] for s in range(spans)]
        parts = swap_blocks(parts, share)
        for g in range(spans):
            r = (g % 2) * half
            out_ref[c, r:r + half, g // 2, :] = parts[g]
    parts = swap_blocks([tback[s] for s in range(spans)], share)
    for k in range(slabs):
        out_ref[k // zdev, bulk:q, k % zdev, :] = parts[k % spans][k // spans:k // spans + 1]


def halves(table):
    high = table.astype(np.float32).astype(ml_dtypes.bfloat16)
    low = (table - high.astype(np.float64)).astype(np.float32).astype(ml_dtypes.bfloat16)
    return np.stack([high, low])


def tables(spans, zdev, q, qp):
    share = LANES // spans
    fourier = fourier_table(spans * zdev)
    order = np.array([s * zdev + z for z in range(zdev) for s in range(spans)])
    basis = np.kron(fourier[order][:, order].T, np.eye(share))
    side = P_SIZE + 1
    matrix = chebyshev_matrix(P_SIZE)
    diff = np.zeros((2 * qp, qp))
    diff[:q, :q] = np.kron(matrix, np.eye(side))
    diff[qp:qp + q, :q] = np.kron(np.eye(side), matrix)
    place = np.zeros((spans * 8, zdev * LANES), ml_dtypes.bfloat16)
    for s in range(spans):
        for z in range(zdev):
            at = z * LANES + s * share
            place[s * 8 + z, at:at + share] = 1.0
    high, low = halves(diff)
    diff = np.concatenate([high, high, low], axis=1)
    place = np.concatenate([place, place], axis=1)
    return halves(basis), diff, place


def vmem(n):
    return [pl.BlockSpec(memory_space=pltpu.VMEM)] * n


def kernels_on_device(spans, planes, adjoint, checkpoints, checkpoint_step, metric,
                      helmholtz_inverse, wall_element, wall_local, wall_weight):
    _, zdev, q, _ = adjoint.shape
    wall_count = wall_element.shape[0]
    qp = -(-q // 16) * 16
    bulk, wide = q - 1, zdev * LANES
    half = bulk // 2
    shape = jax.ShapeDtypeStruct
    basis, diff, place = tables(spans, zdev, q, qp)
    basis, diff, place = jnp.asarray(basis), jnp.asarray(diff), jnp.asarray(place)
    operands = (checkpoint_step, adjoint.transpose(0, 2, 1, 3), checkpoints.transpose(0, 1, 3, 2, 4),
                helmholtz_inverse.transpose(1, 0, 2), metric, wall_element.T, wall_local.T,
                wall_weight, basis, diff, place)
    landing = [pltpu.SMEM(checkpoint_step.shape, jnp.int32)]
    landing += [pltpu.VMEM(a.shape, a.dtype) for a in operands[1:]]
    back, tback, weighted, squares = pl.pallas_call(
        functools.partial(step_kernel, spans, planes, zdev, q, qp),
        out_shape=(shape((3, spans, half, LANES), jnp.int16), shape((spans, 8, LANES), F32),
                   shape((zdev, wall_count // planes), F32),
                   shape((planes, spans, 1, LANES), F32)),
        in_specs=[pl.BlockSpec(memory_space=pl.ANY)] * len(operands),
        out_specs=tuple(vmem(4)),
        scratch_shapes=landing + [
            pltpu.VMEM((qp, 3 * wide), F32),
            pltpu.VMEM((2, qp, wide), F32),
            pltpu.VMEM((NSTEP, 2, q, zdev, LANES), F32),
            pltpu.VMEM((qp, 3 * wide), F32),
            pltpu.VMEM((NSTEP - 1, 2, qp, wide), F32),
            pltpu.VMEM((qp, wide), F32),
            pltpu.VMEM((qp, LANES), F32),
            pltpu.VMEM((zdev, qp, LANES), jnp.int16),
            pltpu.VMEM((zdev, spans, qp, LANES), jnp.int16),
            pltpu.VMEM((spans, 8, LANES), F32),
            pltpu.VMEM((3, spans, half, LANES), jnp.int16),
            pltpu.VMEM((spans, 8, LANES), F32),
            pltpu.VMEM((3, spans, half, LANES), jnp.int16),
            pltpu.VMEM((spans, 8, LANES), F32),
            pltpu.VMEM((NSTEP - 1, spans, bulk, LANES), BF16),
            pltpu.VMEM((NSTEP - 1, spans, bulk, LANES), BF16),
            pltpu.VMEM((spans, half, LANES), BF16),
            pltpu.VMEM((spans, half, LANES), BF16),
            pltpu.VMEM((3 * qp, wide), F32),
            pltpu.VMEM((3 * qp, wide), F32),
            pltpu.VMEM((qp, wide), F32),
            pltpu.VMEM((qp, wide), F32),
            pltpu.VMEM((zdev, spans * qp, 3 * LANES), BF16),
            pltpu.VMEM((3, spans, half, LANES), jnp.int16),
            pltpu.VMEM((spans, 8, LANES), F32),
            pltpu.VMEM((planes, 2, 2 * qp, 2 * LANES), BF16),
            pltpu.VMEM((planes, 2, LANES, 2 * LANES), F32),
            pltpu.VMEM((planes, spans, 8, LANES), F32),
            pltpu.VMEM((planes, spans, 8, LANES), F32),
            pltpu.VMEM((spans, 8, LANES), F32),
            pltpu.VMEM((spans, 8, LANES), F32),
            pltpu.VMEM((1, LANES), F32),
            pltpu.SemaphoreType.DMA((2, 17, spans)),
            pltpu.SemaphoreType.DMA((2, planes * spans)),
            pltpu.SemaphoreType.DMA((len(operands),)),
            pltpu.SemaphoreType.DMA((4 + zdev + NSTEP,)),
        ],
        compiler_params=pltpu.CompilerParams(collective_id=0, has_side_effects=True),
        name="steps",
    )(*operands)
    field, gradient = pl.pallas_call(
        functools.partial(finish_kernel, spans, planes, zdev, q, float(spans * zdev * wall_count)),
        out_shape=(shape((3, q, zdev, LANES), F32), shape((zdev, wall_count // planes), F32)),
        in_specs=vmem(4),
        out_specs=tuple(vmem(2)),
        name="finish",
    )(back, tback, weighted, squares)
    return field.transpose(0, 2, 1, 3), gradient


def chosen(spans, planes, *args):
    zdev, q, elems = args[0].shape[1:]
    walls = args[5].shape[0]
    fits = (
        elems == LANES and spans == 2 * zdev and planes == zdev == 4
        and walls == planes * 2 * LANES and q % 16 == 1 and q < LANES
    )
    if fits:
        return kernels_on_device(spans, planes, *args)
    return on_device(*args)


def solution(mesh):
    placed = (
        P(None, "span", None, "plane"),
        P(None, None, "span", None, "plane"),
        P(),
        P(None, "plane"),
        P("span", None, None),
        P(),
        P(),
        P("span", None),
    )
    return jax.shard_map(
        functools.partial(chosen, mesh.shape["span"], mesh.shape["plane"]),
        mesh=mesh,
        in_specs=placed,
        out_specs=(P(None, "span", None, "plane"), P("span", "plane")),
        check_vma=False,
    )
```

time: 64.1 us -> 52.5 us (0.82)
  Pallas kernels: 58.7 us -> 51.7 us
  local copies, waits for them, and re-layouts: 4.56 us -> 0 us
    pallas_call x1, Pallas kernels: 56.1 us -> 49.1 us  [kernels_on_device(): pl.pallas_call(functools.partial(step_kernel, spans, planes, zdev, q, qp)...]
    unnamed x2 -> x0, local copies, waits for them, and re-layouts: 4.56 us -> none
where the time goes in v1:
time: 52.5 us; the launch traced here: 52.4 us
  Pallas kernels  51.7 us (98%)
  between operations  0.64 us (1%)
    pallas_call x1, Pallas kernels, kernels_on_device(): pl.pallas_call(functools.partial(step_kernel, spans, planes, zdev, q, qp)...  49.1 us
    pallas_call x1, Pallas kernels, kernels_on_device(): pl.pallas_call(functools.partial(finish_kernel, spans, planes, zdev, q, f...  2.59 us

profile of v1, /device:TPU:0, one launch (start us, length us, event | category | flops | bytes accessed | tf_op | source)
XLA Modules:
  0.0 52.4 jit_solution(4739840178603982750)
XLA Ops:
  0.6 49.1 %steps.1 = (s16[3,8,40,128]{3,2,1,0:T(8,128)(2,1)}, f32[8,8,128]{2,1,0:T(8,128)}, f32[4,256]{1,0:T(4,128)}, f32[4,8,1,128]{3,2,1,0:T(1,128)}) custom-call(s32[3]{0:T(128)} %step_h.1, f32[3,81,4,128]{3,2,1,0:T(4,128)} %bitcast.7, bf16[8,2,81,4,128]{4,3,2,1,0:T(4,128)(2,1)} %bitcast.6, f32[81,4,81]{2,1,0:T(4,128)} %bitcast.8, f32[2,128]{1,0:T(2,128)} %metric_h.1, ...), custom_call_target="tpu_custom_call" | custom-call | tf_op jit(solution)/shard_map/steps/pallas_call | solution.py:673
  49.8 2.6 %finish.1 = (f32[3,81,4,128]{3,2,1,0:T(4,128)}, f32[4,256]{1,0:T(4,128)}) custom-call(s16[3,8,40,128]{3,2,1,0:T(8,128)(2,1)} %get-tuple-element.8.back, f32[8,8,128]{2,1,0:T(8,128)} %get-tuple-element.9.tback, f32[4,256]{1,0:T(4,128)} %get-tuple-element.10.weighted_ref, f32[4,8,1,128]{3,2,1,0:T(1,128)} %get-tuple-element.11.srcv), custom_call_target="tpu_custom_call" | custom-call | tf_op jit(solution)/shard_map/finish/pallas_call | solution.py:721

commit v2 on v1

--- a/solution.py
+++ b/solution.py
@@ -132,6 +132,7 @@
 F32 = jnp.float32
 BF16 = jnp.bfloat16
 LANES = 128
+NKINDS = 18
 
 
 def swap_blocks(parts, share):
@@ -199,7 +200,7 @@
                 home, vhome, vf, xs_ref, vs_ref, v0_ref, padded, inv16, modes_ref, tail,
                 snd, tsnd, rcv, trc, vsnd, vrcv, wsnd, wrc,
                 coef, solved, product, kept, modes_cat, bsnd, tbsnd,
-                picks, keeps, wall, rows_in, part, wrcv, square, sems, sqsems, load_sem, local_sem):
+                picks, keeps, wall, rows_in, part, wrcv, square, sems, load_sem, local_sem):
     share = LANES // spans
     me, p = lax.axis_index("span"), lax.axis_index("plane")
     bulk = q - 1
@@ -226,23 +227,26 @@
     def span_to(o):
         return {"span": (me + o) % spans}
 
-    def sem(kind, o):
-        return sems.at[0, kind, o], sems.at[1, kind, o]
+    mate = me + 1 - 2 * (me % 2)
+    to_mate = {"span": mate}
+    most = slice(0, spans - 1)
 
     started = []
 
-    def send(src, dst, kind, o, target):
-        out = remote(src, dst, *sem(kind, o), target)
-        out.start()
-        started.append(out)
-
-    def to_peers(kind, src, dst):
-        incoming = []
+    def send(src, dst, kind, recv, target):
+        remote(src, dst, sems.at[0, kind], sems.at[1, recv], target).start()
+
+    def arrival(dst, recv):
+        return remote(dst, dst, sems.at[0, 0], sems.at[1, recv], to_mate)
+
+    def sent(kind, whole):
+        started.append(remote(whole, whole, sems.at[0, kind], sems.at[1, 0], to_mate))
+
+    def to_peers(kind, src, dst, whole):
         for o in range(1, spans):
-            to, s = (me + o) % spans, (me + spans - o) % spans
-            send(src(to), dst(me), kind, o, span_to(o))
-            incoming.append(remote(src(to), dst(s), *sem(kind, o), span_to(o)))
-        return incoming
+            send(src((me + o) % spans), dst(me), kind, kind, span_to(o))
+        sent(kind, whole)
+        return arrival(whole, kind)
 
     padded[...] = jnp.zeros_like(padded)
     tail[...] = jnp.zeros_like(tail)
@@ -258,6 +262,41 @@
     for j in range(zdev):
         padded[:q, :q] = inv_ref[:, j, :]
         inv16[j] = mode_block(padded[...], eye, q)
+
+    pl.semaphore_wait(barrier, spans * planes - 1)
+
+    xpeer = {"plane": (p + 2) % planes}
+    cpeer = {"plane": p + 1 - 2 * (p % 2)}
+    px = (p + 2) % planes
+    pc = p + 1 - 2 * (p % 2)
+    pcx = (pc + 2) % planes
+    single = NKINDS
+
+    def block_of(i):
+        return (me + spans - i) % spans if i % 2 == 0 else (mate + spans - i + 1) % spans
+
+    for i in range(2, spans, 2):
+        send(inv16.at[p], modes_ref.at[p, me], 0, single + i, span_to(i))
+    send(inv16.at[p], modes_ref.at[p, me], 0, single + 1, to_mate)
+    own = [pltpu.make_async_copy(inv16.at[j], modes_ref.at[j, me], local_sem.at[4 + j]) for j in range(zdev)]
+    for c in own:
+        c.start()
+    for kind in range(4):
+        sent(kind, modes_ref.at[0, most])
+
+    def relay(i):
+        s = block_of(i)
+        block = modes_ref.at[p, s]
+        arrival(block, single + i).wait_recv()
+        if i % 2 == 0:
+            send(block, block, 0, single + i + 1, to_mate)
+        send(block, block, 1, single + spans + i, xpeer)
+        send(block, block, 2, 2, cpeer)
+
+    def relay_across(i):
+        block = modes_ref.at[px, block_of(i)]
+        arrival(block, single + spans + i).wait_recv()
+        send(block, block, 3, 3, cpeer)
 
     for name in ("step", "metric", "adj", "ck", "diff"):
         loads[name].wait()
@@ -292,46 +331,32 @@
     for d in range(spans):
         tsnd[d] = jnp.concatenate([parts[d][:5]] + [scales[c][d] for c in range(3)], axis=0)
 
-    pl.semaphore_wait(barrier, spans * planes - 1)
-
-    xpeer = {"plane": (p + 2) % planes}
-    cpeer = {"plane": p + 1 - 2 * (p % 2)}
-    px = (p + 2) % planes
-    pc = p + 1 - 2 * (p % 2)
-    pcx = (pc + 2) % planes
-    mate = me + 1 - 2 * (me % 2)
-    to_mate = {"span": mate}
-
-    def block_of(i):
-        return (me + spans - i) % spans if i % 2 == 0 else (mate + spans - i + 1) % spans
-
-    mode_in = {}
-    for i in range(2, spans, 2):
-        send(inv16.at[p], modes_ref.at[p, me], 0, i, span_to(i))
-        mode_in[i] = remote(inv16.at[p], modes_ref.at[p, block_of(i)], *sem(0, i), span_to(i))
-    send(inv16.at[p], modes_ref.at[p, me], 0, 1, to_mate)
-    mode_in[1] = remote(inv16.at[p], modes_ref.at[p, mate], *sem(0, 1), to_mate)
-    for i in range(2, spans, 2):
-        s = block_of(i + 1)
-        mode_in[i + 1] = remote(modes_ref.at[p, s], modes_ref.at[p, s], *sem(0, i + 1), to_mate)
     fields = [None] * 3
-    for c in (1, 0):
-        fields[c] = to_peers(4 + c, lambda to: snd.at[c, to], lambda s: rcv.at[c, s])
-    tails = to_peers(7, lambda to: tsnd.at[to], lambda s: trc.at[s])
-    own = []
-    for c in range(3):
-        own.append(pltpu.make_async_copy(snd.at[c, me], rcv.at[c, me], local_sem.at[c]))
-    own.append(pltpu.make_async_copy(tsnd.at[me], trc.at[me], local_sem.at[3]))
-    own += [pltpu.make_async_copy(inv16.at[j], modes_ref.at[j, me], local_sem.at[4 + j]) for j in range(zdev)]
-    for c in own:
-        c.start()
+
+    def send_field(c):
+        fields[c] = to_peers(4 + c, lambda to: snd.at[c, to], lambda s: rcv.at[c, s], rcv.at[c, most])
 
     speeds = [None] * NSTEP
-    for t in range(1, NSTEP):
+
+    def send_speed(t):
         parts = swap_blocks([vf[t, k // zdev, :bulk, k % zdev, :] for k in range(2 * zdev)], share)
         for d in range(spans):
             vsnd[t - 1, d] = parts[d].astype(BF16)
-        speeds[t] = to_peers(7 + t, lambda to: vsnd.at[t - 1, to], lambda s: vrcv.at[t - 1, s])
+        speeds[t] = to_peers(7 + t, lambda to: vsnd.at[t - 1, to], lambda s: vrcv.at[t - 1, s], vrcv.at[t - 1, most])
+
+    relay(2)
+    send_field(1)
+    relay(1)
+    relay(4)
+    send_field(0)
+    tails = to_peers(7, lambda to: tsnd.at[to], lambda s: trc.at[s], trc.at[most])
+    send_speed(1)
+    relay(6)
+    relay(3)
+    send_speed(2)
+    relay(5)
+    relay(7)
+    relay_across(2)
     parts = []
     for g in range(spans):
         r = (g % 2) * half
@@ -339,22 +364,17 @@
     parts = swap_blocks(parts, share)
     for d in range(spans):
         wsnd[d] = parts[d].astype(BF16)
-    speeds[0] = to_peers(10, lambda to: wsnd.at[to], lambda s: wrc.at[s])
-    fields[2] = to_peers(6, lambda to: snd.at[2, to], lambda s: rcv.at[2, s])
+    speeds[0] = to_peers(10, lambda to: wsnd.at[to], lambda s: wrc.at[s], wrc.at[most])
+    send_field(2)
+    for c in range(3):
+        own.append(pltpu.make_async_copy(snd.at[c, me], rcv.at[c, me], local_sem.at[c]))
+    own.append(pltpu.make_async_copy(tsnd.at[me], trc.at[me], local_sem.at[3]))
     vown = [pltpu.make_async_copy(vsnd.at[t, me], vrcv.at[t, me], local_sem.at[4 + zdev + t]) for t in range(NSTEP - 1)]
     vown.append(pltpu.make_async_copy(wsnd.at[me], wrc.at[me], local_sem.at[3 + zdev + NSTEP]))
-    for c in vown:
+    for c in own[zdev:] + vown:
         c.start()
-
-    later = []
-    for i in [2, 1, 4, 6, 3, 5, 7]:
-        mode_in[i].wait_recv()
-        s = block_of(i)
-        if i % 2 == 0:
-            send(modes_ref.at[p, s], modes_ref.at[p, s], 0, i + 1, to_mate)
-        send(modes_ref.at[p, s], modes_ref.at[p, s], 1, i, xpeer)
-        send(modes_ref.at[p, s], modes_ref.at[p, s], 2, i, cpeer)
-        later.append((i, s))
+    for i in (1, 4, 6):
+        relay_across(i)
 
     lane = lax.broadcasted_iota(jnp.int32, (1, LANES), 1)
     rolled = pltpu.roll(metric_ref[...], (LANES - me * share) % LANES, 1)
@@ -380,16 +400,12 @@
     for name in ("basis", "place", "weight"):
         loads[name].wait()
 
-    across, beside, corner = [], [], []
-    for i, s in later:
-        remote(modes_ref.at[p, s], modes_ref.at[px, s], *sem(1, i), xpeer).wait_recv()
-        send(modes_ref.at[px, s], modes_ref.at[px, s], 3, i, cpeer)
-        beside.append(remote(modes_ref.at[p, s], modes_ref.at[pc, s], *sem(2, i), cpeer))
-        corner.append(remote(modes_ref.at[px, s], modes_ref.at[pcx, s], *sem(3, i), cpeer))
+    for i in (3, 5, 7):
+        relay_across(i)
 
     for c in own:
         c.wait()
-    for c in fields[1] + fields[0] + tails:
+    for c in (fields[1], fields[0], tails):
         c.wait_recv()
 
     def unpack(c):
@@ -411,8 +427,8 @@
     unpack(0)
     unpack(1)
 
-    for c in beside + corner:
-        c.wait_recv()
+    for kind, plane in ((2, pc), (3, pcx)):
+        arrival(modes_ref.at[plane, most], kind).wait_recv()
     for j in range(zdev):
         for s in range(spans):
             high, low = split(mode_matrix(modes_ref[j, s], eye, q))
@@ -449,8 +465,7 @@
             xs_ref[:, c * wide:(c + 1) * wide] = y[i * qp:(i + 1) * qp]
 
     def unpack_speed(t):
-        for c in speeds[t]:
-            c.wait_recv()
+        speeds[t].wait_recv()
         parts = swap_blocks([vrcv[t - 1, s].astype(F32) for s in range(spans)], share)
         for k in range(2 * zdev):
             z = k % zdev
@@ -472,8 +487,7 @@
 
     step((0, 1), 2)
 
-    for c in speeds[0]:
-        c.wait_recv()
+    speeds[0].wait_recv()
     parts = swap_blocks([wrc[s].astype(F32) for s in range(spans)], share)
     for g in range(spans):
         z, r = g // 2, (g % 2) * half
@@ -491,11 +505,10 @@
         acc = acc[:, :LANES] + pltpu.roll(acc[:, LANES:], zdev, 0)
         for s in range(spans):
             wall[piece, s] = acc[s * 8:(s + 1) * 8]
-    rows = []
     for o in range(1, planes):
-        to, s = (p + o) % planes, (p + planes - o) % planes
-        send(wall.at[to], rows_in.at[p], 11, o, {"plane": to})
-        rows.append(remote(wall.at[to], rows_in.at[s], *sem(11, o), {"plane": to}))
+        to = (p + o) % planes
+        send(wall.at[to], rows_in.at[p], 11, 11, {"plane": to})
+    sent(11, wall.at[slice(0, planes - 1)])
     rown = pltpu.make_async_copy(wall.at[p], rows_in.at[p], local_sem.at[0])
     rown.start()
 
@@ -503,24 +516,24 @@
     returned = []
     for c in (0, 1):
         scales[c] = coded_component(xs_ref[:, c * wide:(c + 1) * wide], bsnd, c, spans, share, half)
+        returned.append(to_peers(13 + c, lambda to: bsnd.at[c, to], lambda s: back.at[c, s], back.at[c, most]))
+
+    fields[2].wait_recv()
+    unpack(2)
+
+    step((2,), 0)
+
     rown.wait()
-    for c in rows:
-        c.wait_recv()
+    arrival(rows_in.at[slice(0, planes - 1)], 11).wait_recv()
     part[...] = sum(rows_in[s] for s in range(planes))
-    walls = to_peers(12, lambda to: part.at[to], lambda s: wrcv.at[s])
+    walls = to_peers(12, lambda to: part.at[to], lambda s: wrcv.at[s], wrcv.at[most])
     wown = pltpu.make_async_copy(part.at[me], wrcv.at[me], local_sem.at[0])
     wown.start()
-    for c in (0, 1):
-        returned += to_peers(13 + c, lambda to: bsnd.at[c, to], lambda s: back.at[c, s])
-
-    for c in fields[2]:
-        c.wait_recv()
-    unpack(2)
-
-    step((2,), 0)
+
+    step((2,), 1)
+
     wown.wait()
-    for c in walls:
-        c.wait_recv()
+    walls.wait_recv()
     both = sum(wrcv[s] for s in range(spans))
     sums = jnp.concatenate([both[:zdev], both[zdev:]], axis=1)
     weight = weight_ref[:, pl.ds(pl.multiple_of(p * 2 * LANES, 2 * LANES), 2 * LANES)]
@@ -528,21 +541,15 @@
     weighted_ref[...] = weighted
     sq = weighted * weighted
     square[...] = jnp.sum(sq[:, :LANES] + sq[:, LANES:], axis=0, keepdims=True)
-    squares = []
+    where = p * spans + me
     for a in range(planes):
         for o in range(spans):
             if a or o:
-                to = {"plane": (p + a) % planes, "span": (me + o) % spans}
-                n = a * spans + o
-                out = remote(square, srcv.at[p, me], sqsems.at[0, n], sqsems.at[1, n], to)
-                out.start()
-                started.append(out)
-                squares.append(remote(
-                    square, srcv.at[(p + planes - a) % planes, (me + spans - o) % spans],
-                    sqsems.at[0, n], sqsems.at[1, n], to))
-    srcv[p, me] = square[...]
-
-    step((2,), 1)
+                send(square, srcv.at[where], 17, 17, {"plane": (p + a) % planes, "span": (me + o) % spans})
+    others = srcv.at[slice(0, planes * spans - 1)]
+    sent(17, others)
+    srcv[where] = square[...]
+
     step((2,), 2)
 
     scales[2] = coded_component(xs_ref[:, 2 * wide:], bsnd, 2, spans, share, half)
@@ -551,15 +558,14 @@
     parts = swap_blocks([tail[g] for g in range(spans)], share)
     for d in range(spans):
         tbsnd[d] = jnp.concatenate([parts[d][:5]] + [scales[c][d] for c in range(3)], axis=0)
-    returned += to_peers(15, lambda to: bsnd.at[2, to], lambda s: back.at[2, s])
-    returned += to_peers(16, lambda to: tbsnd.at[to], lambda s: tback.at[s])
+    returned.append(to_peers(15, lambda to: bsnd.at[2, to], lambda s: back.at[2, s], back.at[2, most]))
+    returned.append(to_peers(16, lambda to: tbsnd.at[to], lambda s: tback.at[s], tback.at[most]))
     bown = [pltpu.make_async_copy(bsnd.at[c, me], back.at[c, me], local_sem.at[c]) for c in range(3)]
     bown.append(pltpu.make_async_copy(tbsnd.at[me], tback.at[me], local_sem.at[3]))
     for c in bown:
         c.start()
 
-    for c in squares:
-        c.wait_recv()
+    arrival(others, 17).wait_recv()
     for c in bown:
         c.wait()
     for c in returned:
@@ -610,7 +616,7 @@
     bulk = q - 1
     half = bulk // 2
     slabs = 3 * zdev
-    squares = sum(srcv[a, s] for a in range(planes) for s in range(spans))
+    squares = sum(srcv[n] for n in range(planes * spans))
     full = jnp.sum(squares, axis=1, keepdims=True)
     grad_ref[...] = weighted_ref[...] * lax.rsqrt(full / count + 1e-06)
     for c in range(3):
@@ -674,7 +680,7 @@
         functools.partial(step_kernel, spans, planes, zdev, q, qp),
         out_shape=(shape((3, spans, half, LANES), jnp.int16), shape((spans, 8, LANES), F32),
                    shape((zdev, wall_count // planes), F32),
-                   shape((planes, spans, 1, LANES), F32)),
+                   shape((planes * spans, 1, LANES), F32)),
         in_specs=[pl.BlockSpec(memory_space=pl.ANY)] * len(operands),
         out_specs=tuple(vmem(4)),
         scratch_shapes=landing + [
@@ -710,8 +716,7 @@
             pltpu.VMEM((spans, 8, LANES), F32),
             pltpu.VMEM((spans, 8, LANES), F32),
             pltpu.VMEM((1, LANES), F32),
-            pltpu.SemaphoreType.DMA((2, 17, spans)),
-            pltpu.SemaphoreType.DMA((2, planes * spans)),
+            pltpu.SemaphoreType.DMA((2, NKINDS + 2 * spans)),
             pltpu.SemaphoreType.DMA((len(operands),)),
             pltpu.SemaphoreType.DMA((4 + zdev + NSTEP,)),
         ],

time: 52.5 us -> 48.2 us (0.918)
  Pallas kernels: 51.7 us -> 47.4 us
    pallas_call x1, Pallas kernels: 49.1 us -> 44.8 us  [kernels_on_device(): pl.pallas_call(functools.partial(step_kernel, spans, planes, zdev, q, qp)...]
where the time goes in v2:
time: 48.2 us; the launch traced here: 48 us
  Pallas kernels  47.4 us (98%)
  between operations  0.64 us (1%)
    pallas_call x1, Pallas kernels, kernels_on_device(): pl.pallas_call(functools.partial(step_kernel, spans, planes, zdev, q, qp)...  44.8 us
    pallas_call x1, Pallas kernels, kernels_on_device(): pl.pallas_call(functools.partial(finish_kernel, spans, planes, zdev, q, f...  2.59 us

profile of v2, /device:TPU:0, one launch (start us, length us, event | category | flops | bytes accessed | tf_op | source)
XLA Modules:
  0.0 48.0 jit_solution(9748019033374592977)
XLA Ops:
  0.6 44.8 %steps.1 = (s16[3,8,40,128]{3,2,1,0:T(8,128)(2,1)}, f32[8,8,128]{2,1,0:T(8,128)}, f32[4,256]{1,0:T(4,128)}, f32[32,1,128]{2,1,0:T(1,128)}) custom-call(s32[3]{0:T(128)} %step_h.1, f32[3,81,4,128]{3,2,1,0:T(4,128)} %bitcast.7, bf16[8,2,81,4,128]{4,3,2,1,0:T(4,128)(2,1)} %bitcast.6, f32[81,4,81]{2,1,0:T(4,128)} %bitcast.8, f32[2,128]{1,0:T(2,128)} %metric_h.1, ...), custom_call_target="tpu_custom_call" | custom-call | tf_op jit(solution)/shard_map/steps/pallas_call | solution.py:679
  45.4 2.6 %finish.1 = (f32[3,81,4,128]{3,2,1,0:T(4,128)}, f32[4,256]{1,0:T(4,128)}) custom-call(s16[3,8,40,128]{3,2,1,0:T(8,128)(2,1)} %get-tuple-element.8.back, f32[8,8,128]{2,1,0:T(8,128)} %get-tuple-element.9.tback, f32[4,256]{1,0:T(4,128)} %get-tuple-element.10.weighted_ref, f32[32,1,128]{2,1,0:T(1,128)} %get-tuple-element.11.srcv), custom_call_target="tpu_custom_call" | custom-call | tf_op jit(solution)/shard_map/finish/pallas_call | solution.py:726

commit v3 on v2

--- a/solution.py
+++ b/solution.py
@@ -133,6 +133,8 @@
 BF16 = jnp.bfloat16
 LANES = 128
 NKINDS = 18
+ORDER = (2, 6, 1, 7, 4, 3, 5)
+MODE_ROWS = 64
 
 
 def swap_blocks(parts, share):
@@ -177,7 +179,11 @@
     whole = jnp.round(off * (32767.0 * jnp.exp2(-power)))
     for i, extra in enumerate((power, power_d, high, low)):
         whole = jnp.where(row == q + i, extra, whole)
-    return whole.astype(jnp.int32).astype(jnp.int16)
+    lane = lax.broadcasted_iota(jnp.int32, (MODE_ROWS, LANES), 1)
+    rest = whole[MODE_ROWS:MODE_ROWS + 24]
+    aside = jnp.concatenate(
+        [pltpu.roll(rest, q, 1), pltpu.roll(rest, 2 * q - LANES, 1), jnp.zeros((MODE_ROWS - 48, LANES), F32)], axis=0)
+    return jnp.where(lane < q, whole[:MODE_ROWS], aside).astype(jnp.int32).astype(jnp.int16)
 
 
 def power_of(top):
@@ -186,6 +192,10 @@
 
 def mode_matrix(block, eye, q):
     x = block.astype(jnp.int32).astype(F32)
+    lane = lax.broadcasted_iota(jnp.int32, (24, LANES), 1)
+    rest = jnp.where(lane < LANES - q, pltpu.roll(x[:24], LANES - q, 1), pltpu.roll(x[24:48], 2 * (LANES - q), 1))
+    x = jnp.concatenate([x, rest, jnp.zeros((eye.shape[0] - MODE_ROWS - 24, LANES), F32)], axis=0)
+    x = jnp.where(lax.broadcasted_iota(jnp.int32, x.shape, 1) < q, x, 0.0)
     scale = jnp.exp2(x[q:q + 1]) * (1.0 / 32767.0)
     diag = (x[q + 2:q + 3] + x[q + 3:q + 4] * (1.0 / 32767.0)) * (jnp.exp2(x[q + 1:q + 2]) * (1.0 / 32767.0))
     row = lax.broadcasted_iota(jnp.int32, x.shape, 0)
@@ -193,10 +203,10 @@
 
 
 def step_kernel(spans, planes, zdev, q, qp,
-                step_h, adj_h, ck_h, inv_h, metric_h, elem_h, local_h, weight_h, basis_h, diff_h, place_h,
+                step_h, adj_h, ck_h, inv_h, metric_h, elem_h, local_h, weight_h, basis_h, diff_h, place_h, spread_h,
                 back, tback, weighted_ref, srcv,
                 step_ref, adj_ref, ck_ref, inv_ref, metric_ref, elem_ref, local_ref, weight_ref,
-                basis_ref, diff_ref, place_ref,
+                basis_ref, diff_ref, place_ref, spread_ref,
                 home, vhome, vf, xs_ref, vs_ref, v0_ref, padded, inv16, modes_ref, tail,
                 snd, tsnd, rcv, trc, vsnd, vrcv, wsnd, wrc,
                 coef, solved, product, kept, modes_cat, bsnd, tbsnd,
@@ -215,10 +225,10 @@
                 pl.semaphore_signal(
                     barrier, 1, device_id={"plane": (p + a) % planes, "span": (me + o) % spans},
                     device_id_type=MESH)
-    names = ("inv", "step", "metric", "adj", "ck", "diff", "elem", "local", "place", "basis", "weight")
+    names = ("inv", "step", "metric", "adj", "ck", "diff", "elem", "local", "place", "basis", "weight", "spread")
     pairs = ((inv_h, inv_ref), (step_h, step_ref), (metric_h, metric_ref), (adj_h, adj_ref), (ck_h, ck_ref),
              (diff_h, diff_ref), (elem_h, elem_ref), (local_h, local_ref), (place_h, place_ref),
-             (basis_h, basis_ref), (weight_h, weight_ref))
+             (basis_h, basis_ref), (weight_h, weight_ref), (spread_h, spread_ref))
     loads = {}
     for i, (src, dst) in enumerate(pairs):
         loads[names[i]] = pltpu.make_async_copy(src, dst, load_sem.at[i])
@@ -273,11 +283,10 @@
     single = NKINDS
 
     def block_of(i):
-        return (me + spans - i) % spans if i % 2 == 0 else (mate + spans - i + 1) % spans
-
-    for i in range(2, spans, 2):
+        return (me + spans - i) % spans
+
+    for i in ORDER:
         send(inv16.at[p], modes_ref.at[p, me], 0, single + i, span_to(i))
-    send(inv16.at[p], modes_ref.at[p, me], 0, single + 1, to_mate)
     own = [pltpu.make_async_copy(inv16.at[j], modes_ref.at[j, me], local_sem.at[4 + j]) for j in range(zdev)]
     for c in own:
         c.start()
@@ -288,8 +297,6 @@
         s = block_of(i)
         block = modes_ref.at[p, s]
         arrival(block, single + i).wait_recv()
-        if i % 2 == 0:
-            send(block, block, 0, single + i + 1, to_mate)
         send(block, block, 1, single + spans + i, xpeer)
         send(block, block, 2, 2, cpeer)
 
@@ -344,19 +351,17 @@
             vsnd[t - 1, d] = parts[d].astype(BF16)
         speeds[t] = to_peers(7 + t, lambda to: vsnd.at[t - 1, to], lambda s: vrcv.at[t - 1, s], vrcv.at[t - 1, most])
 
-    relay(2)
     send_field(1)
-    relay(1)
-    relay(4)
     send_field(0)
     tails = to_peers(7, lambda to: tsnd.at[to], lambda s: trc.at[s], trc.at[most])
+    for i in ORDER[:4]:
+        relay(i)
     send_speed(1)
-    relay(6)
-    relay(3)
+    for i in ORDER[4:]:
+        relay(i)
     send_speed(2)
-    relay(5)
-    relay(7)
-    relay_across(2)
+    for i in ORDER[:3]:
+        relay_across(i)
     parts = []
     for g in range(spans):
         r = (g % 2) * half
@@ -373,7 +378,7 @@
     vown.append(pltpu.make_async_copy(wsnd.at[me], wrc.at[me], local_sem.at[3 + zdev + NSTEP]))
     for c in own[zdev:] + vown:
         c.start()
-    for i in (1, 4, 6):
+    for i in ORDER[3:5]:
         relay_across(i)
 
     lane = lax.broadcasted_iota(jnp.int32, (1, LANES), 1)
@@ -397,10 +402,10 @@
             pick = jnp.where(local_ref[k:k + 1, lanes] == mode, 1.0, 0.0).astype(BF16)
             picks[piece, k] = jnp.concatenate([pick, pick], axis=0)
             keeps[piece, k] = jnp.where(elem_ref[k:k + 1, lanes] == near, 1.0, 0.0)
-    for name in ("basis", "place", "weight"):
+    for name in ("basis", "place", "weight", "spread"):
         loads[name].wait()
 
-    for i in (3, 5, 7):
+    for i in ORDER[5:]:
         relay_across(i)
 
     for c in own:
@@ -431,10 +436,8 @@
         arrival(modes_ref.at[plane, most], kind).wait_recv()
     for j in range(zdev):
         for s in range(spans):
-            high, low = split(mode_matrix(modes_ref[j, s], eye, q))
-            modes_cat[j, s * qp:(s + 1) * qp, :LANES] = high
-            modes_cat[j, s * qp:(s + 1) * qp, LANES:2 * LANES] = high
-            modes_cat[j, s * qp:(s + 1) * qp, 2 * LANES:] = low
+            both = jnp.concatenate(split(mode_matrix(modes_ref[j, s], eye, q)), axis=1)
+            modes_cat[j, s * qp:(s + 1) * qp, :] = dot(both, spread_ref[...]).astype(BF16)
 
     def step(group, t):
         count = len(group)
@@ -449,12 +452,10 @@
             coef[c * qp:(c + 1) * qp, :] = x
         coef[rows, :] = transform(coef[rows, :], basis_ref, False)
         block = lax.broadcasted_iota(jnp.int32, (1, count * LANES), 1) % LANES // share
-        gap = jnp.zeros((LANES - qp, count * LANES), BF16)
         for j in range(zdev):
             lanes = slice(j * LANES, (j + 1) * LANES)
             x = jnp.concatenate([coef[c * qp:(c + 1) * qp, lanes] for c in group], axis=1)
-            high, low = split(x)
-            r = dot(modes_cat[j], jnp.concatenate([high, gap, low, gap, high, gap], axis=0))
+            r = dot(modes_cat[j], stacked(x, bulk))
             acc = r[:qp]
             for s in range(1, spans):
                 acc = jnp.where(block == s, r[s * qp:(s + 1) * qp], acc)
@@ -527,10 +528,25 @@
     arrival(rows_in.at[slice(0, planes - 1)], 11).wait_recv()
     part[...] = sum(rows_in[s] for s in range(planes))
     walls = to_peers(12, lambda to: part.at[to], lambda s: wrcv.at[s], wrcv.at[most])
-    wown = pltpu.make_async_copy(part.at[me], wrcv.at[me], local_sem.at[0])
+    wown = pltpu.make_async_copy(part.at[me], wrcv.at[me], local_sem.at[4])
     wown.start()
 
     step((2,), 1)
+
+    step((2,), 2)
+
+    scales[2] = coded_component(xs_ref[:, 2 * wide:], bsnd, 2, spans, share, half)
+    for k in range(slabs):
+        tail[k % spans, k // spans:k // spans + 1, :] = xs_ref[bulk:q, k * LANES:(k + 1) * LANES]
+    parts = swap_blocks([tail[g] for g in range(spans)], share)
+    for d in range(spans):
+        tbsnd[d] = jnp.concatenate([parts[d][:5]] + [scales[c][d] for c in range(3)], axis=0)
+    returned.append(to_peers(15, lambda to: bsnd.at[2, to], lambda s: back.at[2, s], back.at[2, most]))
+    returned.append(to_peers(16, lambda to: tbsnd.at[to], lambda s: tback.at[s], tback.at[most]))
+    bown = [pltpu.make_async_copy(bsnd.at[c, me], back.at[c, me], local_sem.at[c]) for c in range(3)]
+    bown.append(pltpu.make_async_copy(tbsnd.at[me], tback.at[me], local_sem.at[3]))
+    for c in bown:
+        c.start()
 
     wown.wait()
     walls.wait_recv()
@@ -550,21 +566,6 @@
     sent(17, others)
     srcv[where] = square[...]
 
-    step((2,), 2)
-
-    scales[2] = coded_component(xs_ref[:, 2 * wide:], bsnd, 2, spans, share, half)
-    for k in range(slabs):
-        tail[k % spans, k // spans:k // spans + 1, :] = xs_ref[bulk:q, k * LANES:(k + 1) * LANES]
-    parts = swap_blocks([tail[g] for g in range(spans)], share)
-    for d in range(spans):
-        tbsnd[d] = jnp.concatenate([parts[d][:5]] + [scales[c][d] for c in range(3)], axis=0)
-    returned.append(to_peers(15, lambda to: bsnd.at[2, to], lambda s: back.at[2, s], back.at[2, most]))
-    returned.append(to_peers(16, lambda to: tbsnd.at[to], lambda s: tback.at[s], tback.at[most]))
-    bown = [pltpu.make_async_copy(bsnd.at[c, me], back.at[c, me], local_sem.at[c]) for c in range(3)]
-    bown.append(pltpu.make_async_copy(tbsnd.at[me], tback.at[me], local_sem.at[3]))
-    for c in bown:
-        c.start()
-
     arrival(others, 17).wait_recv()
     for c in bown:
         c.wait()
@@ -574,9 +575,17 @@
         c.wait_send()
 
 
+def stacked(x, bulk):
+    high, low = split(x)
+    row = lax.broadcasted_iota(jnp.int32, (16, x.shape[1]), 0)
+    last = x[bulk:bulk + 1]
+    last_high = last.astype(BF16).astype(F32)
+    ends = jnp.where(row == 1, last - last_high, jnp.where(row < 3, last_high, 0.0)).astype(BF16)
+    return jnp.concatenate([high[:bulk], low[:bulk], high[:bulk], ends], axis=0)
+
+
 def transport_block(x, v0, v1, diff_ref, qp):
-    high, low = split(x)
-    d = dot(diff_ref[...], jnp.concatenate([high, low, high], axis=0))
+    d = dot(diff_ref[...], stacked(x, qp - 16))
     return x + v0 * d[:qp] + v1 * d[qp:]
 
 
@@ -651,10 +660,17 @@
         for z in range(zdev):
             at = z * LANES + s * share
             place[s * 8 + z, at:at + share] = 1.0
+    bulk = q - 1
+    spread = np.zeros((2 * LANES, 2 * LANES), ml_dtypes.bfloat16)
+    for i in range(bulk):
+        spread[i, i] = spread[i, bulk + i] = spread[LANES + i, 2 * bulk + i] = 1.0
+    spread[bulk, 3 * bulk] = spread[bulk, 3 * bulk + 1] = spread[LANES + bulk, 3 * bulk + 2] = 1.0
     high, low = halves(diff)
-    diff = np.concatenate([high, high, low], axis=1)
+    gap = np.zeros((2 * qp, LANES - qp), ml_dtypes.bfloat16)
+    diff = np.concatenate([high, gap, low, gap], axis=1).astype(np.float32) @ spread.astype(np.float32)
+    diff = diff.astype(ml_dtypes.bfloat16)
     place = np.concatenate([place, place], axis=1)
-    return halves(basis), diff, place
+    return halves(basis), diff, place, spread
 
 
 def vmem(n):
@@ -669,11 +685,10 @@
     bulk, wide = q - 1, zdev * LANES
     half = bulk // 2
     shape = jax.ShapeDtypeStruct
-    basis, diff, place = tables(spans, zdev, q, qp)
-    basis, diff, place = jnp.asarray(basis), jnp.asarray(diff), jnp.asarray(place)
+    constants = [jnp.asarray(a) for a in tables(spans, zdev, q, qp)]
     operands = (checkpoint_step, adjoint.transpose(0, 2, 1, 3), checkpoints.transpose(0, 1, 3, 2, 4),
                 helmholtz_inverse.transpose(1, 0, 2), metric, wall_element.T, wall_local.T,
-                wall_weight, basis, diff, place)
+                wall_weight, *constants)
     landing = [pltpu.SMEM(checkpoint_step.shape, jnp.int32)]
     landing += [pltpu.VMEM(a.shape, a.dtype) for a in operands[1:]]
     back, tback, weighted, squares = pl.pallas_call(
@@ -691,8 +706,8 @@
             pltpu.VMEM((NSTEP - 1, 2, qp, wide), F32),
             pltpu.VMEM((qp, wide), F32),
             pltpu.VMEM((qp, LANES), F32),
-            pltpu.VMEM((zdev, qp, LANES), jnp.int16),
-            pltpu.VMEM((zdev, spans, qp, LANES), jnp.int16),
+            pltpu.VMEM((zdev, MODE_ROWS, LANES), jnp.int16),
+            pltpu.VMEM((zdev, spans, MODE_ROWS, LANES), jnp.int16),
             pltpu.VMEM((spans, 8, LANES), F32),
             pltpu.VMEM((3, spans, half, LANES), jnp.int16),
             pltpu.VMEM((spans, 8, LANES), F32),
@@ -706,7 +721,7 @@
             pltpu.VMEM((3 * qp, wide), F32),
             pltpu.VMEM((qp, wide), F32),
             pltpu.VMEM((qp, wide), F32),
-            pltpu.VMEM((zdev, spans * qp, 3 * LANES), BF16),
+            pltpu.VMEM((zdev, spans * qp, 2 * LANES), BF16),
             pltpu.VMEM((3, spans, half, LANES), jnp.int16),
             pltpu.VMEM((spans, 8, LANES), F32),
             pltpu.VMEM((planes, 2, 2 * qp, 2 * LANES), BF16),
@@ -738,7 +753,7 @@
     walls = args[5].shape[0]
     fits = (
         elems == LANES and spans == 2 * zdev and planes == zdev == 4
-        and walls == planes * 2 * LANES and q % 16 == 1 and q < LANES
+        and walls == planes * 2 * LANES and q == (P_SIZE + 1) ** 2 and MODE_ROWS < q < 85
     )
     if fits:
         return kernels_on_device(spans, planes, *args)

time: 48.2 us -> 47.2 us (0.979)
  Pallas kernels: 47.4 us -> 46.4 us
    pallas_call x1, Pallas kernels: 44.8 us -> 43.8 us  [kernels_on_device(): pl.pallas_call(functools.partial(step_kernel, spans, planes, zdev, q, qp)...]
where the time goes in v3:
time: 47.2 us; the launch traced here: 47 us
  Pallas kernels  46.4 us (98%)
  between operations  0.64 us (1%)
    pallas_call x1, Pallas kernels, kernels_on_device(): pl.pallas_call(functools.partial(step_kernel, spans, planes, zdev, q, qp)...  43.8 us
    pallas_call x1, Pallas kernels, kernels_on_device(): pl.pallas_call(functools.partial(finish_kernel, spans, planes, zdev, q, f...  2.59 us

profile of v3, /device:TPU:0, one launch (start us, length us, event | category | flops | bytes accessed | tf_op | source)
XLA Modules:
  0.0 47.0 jit_solution(10782478044148526827)
XLA Ops:
  0.6 43.8 %steps.1 = (s16[3,8,40,128]{3,2,1,0:T(8,128)(2,1)}, f32[8,8,128]{2,1,0:T(8,128)}, f32[4,256]{1,0:T(4,128)}, f32[32,1,128]{2,1,0:T(1,128)}) custom-call(s32[3]{0:T(128)} %step_h.1, f32[3,81,4,128]{3,2,1,0:T(4,128)} %bitcast.7, bf16[8,2,81,4,128]{4,3,2,1,0:T(4,128)(2,1)} %bitcast.6, f32[81,4,81]{2,1,0:T(4,128)} %bitcast.8, f32[2,128]{1,0:T(2,128)} %metric_h.1, ...), custom_call_target="tpu_custom_call" | custom-call | tf_op jit(solution)/shard_map/steps/pallas_call | solution.py:694
  44.4 2.6 %finish.1 = (f32[3,81,4,128]{3,2,1,0:T(4,128)}, f32[4,256]{1,0:T(4,128)}) custom-call(s16[3,8,40,128]{3,2,1,0:T(8,128)(2,1)} %get-tuple-element.8.back, f32[8,8,128]{2,1,0:T(8,128)} %get-tuple-element.9.tback, f32[4,256]{1,0:T(4,128)} %get-tuple-element.10.weighted_ref, f32[32,1,128]{2,1,0:T(1,128)} %get-tuple-element.11.srcv), custom_call_target="tpu_custom_call" | custom-call | tf_op jit(solution)/shard_map/finish/pallas_call | solution.py:741

commit v4 on v3

--- a/solution.py
+++ b/solution.py
@@ -345,10 +345,12 @@
 
     speeds = [None] * NSTEP
 
-    def send_speed(t):
+    def pack_speed(t):
         parts = swap_blocks([vf[t, k // zdev, :bulk, k % zdev, :] for k in range(2 * zdev)], share)
         for d in range(spans):
             vsnd[t - 1, d] = parts[d].astype(BF16)
+
+    def send_speed(t):
         speeds[t] = to_peers(7 + t, lambda to: vsnd.at[t - 1, to], lambda s: vrcv.at[t - 1, s], vrcv.at[t - 1, most])
 
     send_field(1)
@@ -356,10 +358,11 @@
     tails = to_peers(7, lambda to: tsnd.at[to], lambda s: trc.at[s], trc.at[most])
     for i in ORDER[:4]:
         relay(i)
+    pack_speed(1)
     send_speed(1)
     for i in ORDER[4:]:
         relay(i)
-    send_speed(2)
+    pack_speed(2)
     for i in ORDER[:3]:
         relay_across(i)
     parts = []
@@ -369,8 +372,6 @@
     parts = swap_blocks(parts, share)
     for d in range(spans):
         wsnd[d] = parts[d].astype(BF16)
-    speeds[0] = to_peers(10, lambda to: wsnd.at[to], lambda s: wrc.at[s], wrc.at[most])
-    send_field(2)
     for c in range(3):
         own.append(pltpu.make_async_copy(snd.at[c, me], rcv.at[c, me], local_sem.at[c]))
     own.append(pltpu.make_async_copy(tsnd.at[me], trc.at[me], local_sem.at[3]))
@@ -412,6 +413,7 @@
         c.wait()
     for c in (fields[1], fields[0], tails):
         c.wait_recv()
+    send_speed(2)
 
     def unpack(c):
         parts = [rcv[c, s].astype(jnp.int32).astype(F32) * trc[s, 5 + c:6 + c, :] for s in range(spans)]
@@ -475,6 +477,8 @@
     one = slice(wide, 2 * wide)
 
     step((0, 1), 0)
+    speeds[0] = to_peers(10, lambda to: wsnd.at[to], lambda s: wrc.at[s], wrc.at[most])
+    send_field(2)
     kept[...] = xs_ref[:, one]
 
     for c in vown:
@@ -514,10 +518,15 @@
     rown.start()
 
     scales = [None] * 3
-    returned = []
+    returned = [None] * 3
+
+    def give_back(c):
+        returned[c] = to_peers(13 + c, lambda to: bsnd.at[c, to], lambda s: back.at[c, s], back.at[c, most])
+
     for c in (0, 1):
         scales[c] = coded_component(xs_ref[:, c * wide:(c + 1) * wide], bsnd, c, spans, share, half)
-        returned.append(to_peers(13 + c, lambda to: bsnd.at[c, to], lambda s: back.at[c, s], back.at[c, most]))
+        if c == 0:
+            give_back(c)
 
     fields[2].wait_recv()
     unpack(2)
@@ -530,6 +539,7 @@
     walls = to_peers(12, lambda to: part.at[to], lambda s: wrcv.at[s], wrcv.at[most])
     wown = pltpu.make_async_copy(part.at[me], wrcv.at[me], local_sem.at[4])
     wown.start()
+    give_back(1)
 
     step((2,), 1)
 
@@ -541,12 +551,6 @@
     parts = swap_blocks([tail[g] for g in range(spans)], share)
     for d in range(spans):
         tbsnd[d] = jnp.concatenate([parts[d][:5]] + [scales[c][d] for c in range(3)], axis=0)
-    returned.append(to_peers(15, lambda to: bsnd.at[2, to], lambda s: back.at[2, s], back.at[2, most]))
-    returned.append(to_peers(16, lambda to: tbsnd.at[to], lambda s: tback.at[s], tback.at[most]))
-    bown = [pltpu.make_async_copy(bsnd.at[c, me], back.at[c, me], local_sem.at[c]) for c in range(3)]
-    bown.append(pltpu.make_async_copy(tbsnd.at[me], tback.at[me], local_sem.at[3]))
-    for c in bown:
-        c.start()
 
     wown.wait()
     walls.wait_recv()
@@ -566,10 +570,17 @@
     sent(17, others)
     srcv[where] = square[...]
 
+    tailed = to_peers(16, lambda to: tbsnd.at[to], lambda s: tback.at[s], tback.at[most])
+    give_back(2)
+    bown = [pltpu.make_async_copy(bsnd.at[c, me], back.at[c, me], local_sem.at[c]) for c in range(3)]
+    bown.append(pltpu.make_async_copy(tbsnd.at[me], tback.at[me], local_sem.at[3]))
+    for c in bown:
+        c.start()
+
     arrival(others, 17).wait_recv()
     for c in bown:
         c.wait()
-    for c in returned:
+    for c in returned + [tailed]:
         c.wait_recv()
     for c in started:
         c.wait_send()
@@ -689,6 +700,7 @@
     operands = (checkpoint_step, adjoint.transpose(0, 2, 1, 3), checkpoints.transpose(0, 1, 3, 2, 4),
                 helmholtz_inverse.transpose(1, 0, 2), metric, wall_element.T, wall_local.T,
                 wall_weight, *constants)
+    operands = tuple(pltpu.with_memory_space_constraint(a, pltpu.HBM) for a in operands)
     landing = [pltpu.SMEM(checkpoint_step.shape, jnp.int32)]
     landing += [pltpu.VMEM(a.shape, a.dtype) for a in operands[1:]]
     back, tback, weighted, squares = pl.pallas_call(
@@ -696,7 +708,7 @@
         out_shape=(shape((3, spans, half, LANES), jnp.int16), shape((spans, 8, LANES), F32),
                    shape((zdev, wall_count // planes), F32),
                    shape((planes * spans, 1, LANES), F32)),
-        in_specs=[pl.BlockSpec(memory_space=pl.ANY)] * len(operands),
+        in_specs=[pl.BlockSpec(memory_space=pltpu.HBM)] * len(operands),
         out_specs=tuple(vmem(4)),
         scratch_shapes=landing + [
             pltpu.VMEM((qp, 3 * wide), F32),
@@ -735,7 +747,7 @@
             pltpu.SemaphoreType.DMA((len(operands),)),
             pltpu.SemaphoreType.DMA((4 + zdev + NSTEP,)),
         ],
-        compiler_params=pltpu.CompilerParams(collective_id=0, has_side_effects=True),
+        compiler_params=pltpu.CompilerParams(collective_id=0, has_side_effects=True, vmem_limit_bytes=24 << 20),
         name="steps",
     )(*operands)
     field, gradient = pl.pallas_call(
@@ -743,6 +755,7 @@
         out_shape=(shape((3, q, zdev, LANES), F32), shape((zdev, wall_count // planes), F32)),
         in_specs=vmem(4),
         out_specs=tuple(vmem(2)),
+        compiler_params=pltpu.CompilerParams(vmem_limit_bytes=8 << 20),
         name="finish",
     )(back, tback, weighted, squares)
     return field.transpose(0, 2, 1, 3), gradient

time: 47.2 us -> 44.1 us (0.934)
  Pallas kernels: 46.4 us -> 43.3 us
    pallas_call x1, Pallas kernels: 43.8 us -> 41.7 us  [kernels_on_device(): pl.pallas_call(functools.partial(step_kernel, spans, planes, zdev, q, qp)...]
    pallas_call x1, Pallas kernels: 2.59 us -> 1.62 us  [kernels_on_device(): pl.pallas_call(functools.partial(finish_kernel, spans, planes, zdev, q, f...]
where the time goes in v4:
time: 44.1 us; the launch traced here: 44 us
  Pallas kernels  43.3 us (98%)
  between operations  0.64 us (1%)
    pallas_call x1, Pallas kernels, kernels_on_device(): pl.pallas_call(functools.partial(step_kernel, spans, planes, zdev, q, qp)...  41.7 us
    pallas_call x1, Pallas kernels, kernels_on_device(): pl.pallas_call(functools.partial(finish_kernel, spans, planes, zdev, q, f...  1.62 us

profile of v4, /device:TPU:0, one launch (start us, length us, event | category | flops | bytes accessed | tf_op | source)
XLA Modules:
  0.0 44.0 jit_solution(2209525250587406574)
XLA Ops:
  0.6 41.7 %steps.1 = (s16[3,8,40,128]{3,2,1,0:T(8,128)(2,1)S(1)}, f32[8,8,128]{2,1,0:T(8,128)S(1)}, f32[4,256]{1,0:T(4,128)S(1)}, f32[32,1,128]{2,1,0:T(1,128)S(1)}) custom-call(s32[3]{0:T(128)} %step_h.1, f32[3,81,4,128]{3,2,1,0:T(4,128)} %bitcast.7, bf16[8,2,81,4,128]{4,3,2,1,0:T(4,128)(2,1)} %bitcast.6, f32[81,4,81]{2,1,0:T(4,128)} %bitcast.8, f32[2,128]{1,0:T(2,128)} %metric_h.1, ...), custom_call_target="tpu_custom_call" | custom-call | tf_op jit(solution)/shard_map/steps/pallas_call | solution.py:706
  42.3 1.6 %finish.1 = (f32[3,81,4,128]{3,2,1,0:T(4,128)}, f32[4,256]{1,0:T(4,128)}) custom-call(s16[3,8,40,128]{3,2,1,0:T(8,128)(2,1)S(1)} %get-tuple-element.8.back, f32[8,8,128]{2,1,0:T(8,128)S(1)} %get-tuple-element.9.tback, f32[4,256]{1,0:T(4,128)S(1)} %get-tuple-element.10.weighted_ref, f32[32,1,128]{2,1,0:T(1,128)S(1)} %get-tuple-element.11.srcv), custom_call_target="tpu_custom_call" | custom-call | tf_op jit(solution)/shard_map/finish/pallas_call | solution.py:753
